TPU v7x, 32 devices: a whole 2x2x4 slice. The times are simulated.
32 devices in a mesh: outer: 4 (over y, core), inner: 8 (over z, x).
Axes of the slice: x: 2, y: 2, z: 4, core: 2. Of those that a mesh axis runs over, the one named last changes fastest.
Arguments:
- queries: bfloat16 [16384, 16, 128], P(('outer', 'inner')), may hold values from -1.5 to 1.5
- key_vectors: bfloat16 [16384, 16, 128], P(('outer', 'inner')), may hold values from -1.5 to 1.5
- value_vectors: bfloat16 [16384, 16, 128], P(('outer', 'inner')), may hold values from -6 to 6
- level_weights: float32 [18, 16, 16384], P(None, None, ('outer', 'inner')), may hold values from 0.25 to 1
Outputs:
- attended: bfloat16 [16384, 16, 128], P(('outer', 'inner'))
All inputs are finite; a program needn't handle non-finite values.
Results may differ from a plain program's by a relative error of at most 0.0049.
Values may be sent and summed in bfloat16 or wider, within the bound.
No kernel may reach another device: no remote copies, remote signals or barrier semaphores. Data moves between devices by JAX's collectives and lax.ppermute only.
A program may use at most 128 MiB of HBM per device.

v0:
```python
import functools
import jax
import jax.numpy as jnp
from jax import lax
from jax.experimental import pallas as pl
from jax.experimental.pallas import tpu as pltpu
from jax.sharding import PartitionSpec as P

AXES = ("outer", "inner")
HEAD_BLOCK = 8
STATE_VMEM = 14 << 20
LOCAL_VMEM = 14 << 20
MERGE_VMEM = 16 << 20
FINAL_VMEM = 14 << 20
MERGE_SPACE = pltpu.VMEM
SPLIT = 3
F32, BF16 = jnp.float32, jnp.bfloat16


def dot_nt(a, b):
    return lax.dot_general(a, b, (((1,), (1,)), ((), ())), preferred_element_type=F32)


def scalar_grid(grid, in_specs, out_specs):
    return pltpu.PrefetchScalarGridSpec(
        num_scalar_prefetch=1, grid=grid, in_specs=in_specs, out_specs=out_specs
    )


def state_kernel(place_ref, k_ref, v_ref, state_ref, first_ref):
    half = k_ref.shape[0] // 2
    quarter = k_ref.shape[1] // 2
    flip = place_ref[0] & 1
    keys = jnp.swapaxes(k_ref[...], 0, 1)
    values = jnp.swapaxes(v_ref[...], 0, 1)
    for h in range(2 * quarter):
        turned = values[h].T
        first = jnp.dot(turned[:, :half], keys[h, :half], preferred_element_type=F32)
        rest = jnp.dot(turned[:, half:], keys[h, half:], preferred_element_type=F32)
        spot = (h // quarter ^ flip) * quarter + h % quarter
        first_ref[spot] = first.astype(BF16)
        state_ref[spot] = (first + rest).astype(BF16)


def block_states(place, key_vectors, value_vectors):
    tokens, heads, dim = key_vectors.shape
    block = heads // 2
    source = pl.BlockSpec((tokens, block, dim), lambda i, p: (0, i ^ (p[0] >> 1 & 1), 0))
    shape = jax.ShapeDtypeStruct((heads, dim, dim), BF16)
    return pl.pallas_call(
        state_kernel,
        grid_spec=scalar_grid(
            (2,),
            [source, source],
            [pl.BlockSpec((block, dim, dim), lambda i, p: (i, 0, 0))] * 2,
        ),
        out_shape=[shape, shape],
        name="states",
        compiler_params=pltpu.CompilerParams(vmem_limit_bytes=STATE_VMEM),
        cost_estimate=pl.CostEstimate(
            flops=2 * tokens * heads * dim * dim,
            bytes_accessed=4 * tokens * heads * dim,
            transcendentals=0,
        ),
    )(place, key_vectors, value_vectors)


def local_kernel(start, blocks, place_ref, q_ref, k_ref, v_ref, w_ref, first_ref, acc_ref, qh_ref):
    unit = start + pl.program_id(0)
    second = (unit >= blocks).astype(F32)
    tile = q_ref.shape[0]
    depth = tile.bit_length() - 1
    groups = tile // 8
    queries = jnp.swapaxes(q_ref[...], 0, 1)
    keys = jnp.swapaxes(k_ref[...], 0, 1)
    values = jnp.swapaxes(v_ref[...], 0, 1)
    heads = queries.shape[0]
    lane = lax.broadcasted_iota(jnp.int32, (8, tile), 1)
    row = lax.broadcasted_iota(jnp.int32, (8, tile), 0)
    fine = (lane & 7) ^ row
    fine_ok = row <= (lane & 7)
    group_lane = lax.broadcasted_iota(jnp.int32, (groups, tile), 1) >> 3
    group_row = lax.broadcasted_iota(jnp.int32, (groups, tile), 0)
    coarse = jnp.where(group_row < group_lane, group_lane ^ group_row, 0)

    def gain(l, h):
        return w_ref[l, h : h + 1, :] * (2.0 ** (-0.5 * l))

    def weigh(h, scores):
        near = jnp.where(fine == 0, gain(0, h), 0.0)
        for l in range(1, 4):
            near = jnp.where((fine >> (l - 1)) == 1, gain(l, h), near)
        near = jnp.where(fine_ok, near, 0.0)
        far = jnp.zeros((groups, tile), F32)
        for l in range(4, depth + 1):
            far = jnp.where((coarse >> (l - 4)) == 1, gain(l, h), far)
        rows = []
        for g in range(0, groups, 2):
            pair = [
                jnp.where(
                    (lane >> 3) == g + i,
                    near,
                    jnp.broadcast_to(far[g + i : g + i + 1, :], (8, tile)),
                )
                * scores[8 * (g + i) : 8 * (g + i) + 8, :]
                for i in range(2)
            ]
            rows.append(jnp.concatenate(pair, axis=0).astype(BF16))
        return jnp.concatenate(rows, axis=0)

    scores, weights = {}, {}
    for h in range(heads + 2):
        if h < heads:
            scores[h] = dot_nt(keys[h], queries[h])
            qh_ref[h] = queries[h]
        if 0 <= h - 1 < heads:
            weights[h - 1] = weigh(h - 1, scores.pop(h - 1))
        if h - 2 >= 0:
            n = h - 2
            out = jnp.dot(values[n].T, weights.pop(n), preferred_element_type=F32)
            last = [(depth + 1, 2.0 ** (-0.5 * (depth + 1)) * second)]
            acc_ref[n] = out + bucket_sum(
                place_ref[0], unit % blocks, w_ref, queries, n, [first_ref], [last]
            )


def local_part(start, count, place, queries, key_vectors, value_vectors, level_weights, first):
    tokens, heads, dim = queries.shape
    tile = tokens // 2
    blocks = heads // HEAD_BLOCK
    source = pl.BlockSpec(
        (tile, HEAD_BLOCK, dim), lambda i, p: ((start + i) // blocks, (start + i) % blocks, 0)
    )
    return pl.pallas_call(
        functools.partial(local_kernel, start, blocks),
        grid_spec=scalar_grid(
            (count,),
            [
                source,
                source,
                source,
                pl.BlockSpec(
                    (level_weights.shape[0], HEAD_BLOCK, tile),
                    lambda i, p: (0, (start + i) % blocks, (start + i) // blocks),
                ),
                pl.BlockSpec((heads, dim, dim), lambda i, p: (0, 0, 0)),
            ],
            [
                pl.BlockSpec((None, HEAD_BLOCK, dim, tile), lambda i, p: (i, 0, 0, 0)),
                pl.BlockSpec((None, HEAD_BLOCK, tile, dim), lambda i, p: (i, 0, 0, 0)),
            ],
        ),
        out_shape=[
            pltpu.HBM((count, HEAD_BLOCK, dim, tile), F32),
            pltpu.HBM((count, HEAD_BLOCK, tile, dim), BF16),
        ],
        compiler_params=pltpu.CompilerParams(vmem_limit_bytes=LOCAL_VMEM),
        cost_estimate=pl.CostEstimate(
            flops=4 * count * tile * tile * HEAD_BLOCK * dim,
            bytes_accessed=12 * count * tile * HEAD_BLOCK * dim,
            transcendentals=0,
        ),
    )(place, queries, key_vectors, value_vectors, level_weights, first)


def gain_row(place, level, bit):
    scale = 2.0 ** (-0.5 * level)
    return [(level, scale if bit is None else scale * (place >> bit & 1).astype(F32))]


def bucket_sum(place, block, w_ref, q_ref, h, refs, rows):
    quarter = refs[0].shape[0] // 4
    spot = block * q_ref.shape[0] + h
    stack = [ref[(spot // quarter ^ (place & 3)) * quarter + spot % quarter] for ref in refs]
    wide = dot_nt(jnp.concatenate(stack, axis=0), q_ref[h])
    dim = stack[0].shape[0]
    total = None
    for n, row in enumerate(rows):
        gain = sum(w_ref[l, h : h + 1, :] * c for l, c in row)
        part = wide[n * dim : (n + 1) * dim] * gain
        total = part if total is None else total + part
    return total


def merge_kernel(levels, blocks, split, place_ref, qa_ref, qb_ref, aa_ref, ab_ref, w_ref, *rest):
    refs, (acc_ref, qh_ref) = rest[:-2], rest[-2:]
    rows = [gain_row(place_ref[0], *level) for level in levels]
    unit = pl.program_id(0)

    def take(q_ref, a_ref):
        qh_ref[...] = q_ref[...]
        for h in range(q_ref.shape[0]):
            acc_ref[h] = a_ref[h] + bucket_sum(
                place_ref[0], unit % blocks, w_ref, q_ref, h, refs, rows
            )

    pl.when(unit < split)(lambda: take(qa_ref, aa_ref))
    pl.when(unit >= split)(lambda: take(qb_ref, ab_ref))


def merge_part(place, turned, accs, level_weights, buckets, levels):
    split, block, tile, dim = turned[0].shape
    units = split + turned[1].shape[0]
    blocks = units // 2
    heads = block * blocks
    ahead = lambda i, p: (jnp.minimum(i, split - 1), 0, 0, 0)
    after = lambda i, p: (jnp.maximum(i - split, 0), 0, 0, 0)
    each = lambda i, p: (i, 0, 0, 0)
    return pl.pallas_call(
        functools.partial(merge_kernel, levels, blocks, split),
        grid_spec=scalar_grid(
            (units,),
            [
                pl.BlockSpec((None, block, tile, dim), ahead),
                pl.BlockSpec((None, block, tile, dim), after),
                pl.BlockSpec((None, block, dim, tile), ahead),
                pl.BlockSpec((None, block, dim, tile), after),
                pl.BlockSpec(
                    (level_weights.shape[0], block, tile), lambda i, p: (0, i % blocks, i // blocks)
                ),
            ]
            + [pl.BlockSpec((heads, dim, dim), lambda i, p: (0, 0, 0))] * len(buckets),
            [
                pl.BlockSpec((None, block, dim, tile), each),
                pl.BlockSpec((None, block, tile, dim), each),
            ],
        ),
        out_shape=[
            MERGE_SPACE((units, block, dim, tile), F32),
            MERGE_SPACE((units, block, tile, dim), BF16),
        ],
        name="merge",
        compiler_params=pltpu.CompilerParams(vmem_limit_bytes=MERGE_VMEM),
        cost_estimate=pl.CostEstimate(
            flops=2 * len(buckets) * units * block * tile * dim * dim,
            bytes_accessed=12 * units * block * tile * dim,
            transcendentals=0,
        ),
    )(place, *turned, *accs, level_weights, *buckets)


def final_kernel(meta, place_ref, q_ref, a_ref, w_ref, *rest):
    refs, out_ref = rest[:-1], rest[-1]
    above, low, top, blocks = meta
    place = place_ref[0]
    bit = lambda g: (place >> g & 1).astype(F32)
    level = lambda g, c: (above + g, c * 2.0 ** (-0.5 * (above + g)))
    rows = [gain_row(place, above + g, g) for g in range(2, top) if g != low]
    rows.append([level(low, bit(low)), level(top, bit(top) * (1.0 - bit(low)))])
    rows.append([level(top, bit(top) * bit(low))])
    done = []
    for h in range(q_ref.shape[0]):
        total = a_ref[h] + bucket_sum(
            place, pl.program_id(0) % blocks, w_ref, q_ref, h, refs, rows
        )
        done.append(total.T.astype(BF16))
    out_ref[...] = jnp.swapaxes(jnp.stack(done), 0, 1)


def final_part(place, turned, acc, level_weights, buckets, low, top):
    units, block, tile, dim = turned.shape
    blocks = units // 2
    heads = block * blocks
    each = lambda i, p: (i, 0, 0, 0)
    return pl.pallas_call(
        functools.partial(final_kernel, ((2 * tile).bit_length(), low, top, blocks)),
        grid_spec=scalar_grid(
            (units,),
            [
                pl.BlockSpec((None, block, tile, dim), each),
                pl.BlockSpec((None, block, dim, tile), each),
                pl.BlockSpec(
                    (level_weights.shape[0], block, tile), lambda i, p: (0, i % blocks, i // blocks)
                ),
            ]
            + [pl.BlockSpec((heads, dim, dim), lambda i, p: (0, 0, 0))] * len(buckets),
            pl.BlockSpec((tile, block, dim), lambda i, p: (i // blocks, i % blocks, 0)),
        ),
        out_shape=jax.ShapeDtypeStruct((2 * tile, heads, dim), BF16),
        name="final",
        compiler_params=pltpu.CompilerParams(vmem_limit_bytes=FINAL_VMEM),
        cost_estimate=pl.CostEstimate(
            flops=2 * len(buckets) * units * block * tile * dim * dim,
            bytes_accessed=12 * units * block * tile * dim,
            transcendentals=0,
        ),
    )(place, turned, acc, level_weights, *buckets)


def exchange(value, mask):
    total = lax.axis_size("outer") * lax.axis_size("inner")
    pairs = [(i, i ^ mask) for i in range(total)]
    return lax.ppermute(value, AXES, pairs)


def exchange_states(state, place, inner_depth, depth):
    quarter = state.shape[0] // 4
    high = (place >> 1 & 1) == 1
    part = lambda m: state[m * quarter : (m + 1) * quarter]
    got = {m: exchange(part(m), m) for m in (3, 2, 1)}
    rest = exchange(jnp.concatenate([part(0), part(2), part(3)]), 1)
    zero = jnp.concatenate([got[1], rest[:quarter], rest[2 * quarter :], rest[quarter : -quarter]])
    mine = part(0).astype(F32) + got[1].astype(F32)
    other = got[2].astype(F32) + got[3].astype(F32)
    total = mine + other
    sent = total.astype(BF16)
    pieces = {1: jnp.where(high, other, mine).astype(BF16)}
    pieces[1], sent, total = lax.optimization_barrier((pieces[1], sent, total))
    for g in range(2, depth):
        pieces[g] = exchange(sent, 1 << g)
        total = total + pieces[g].astype(F32)
        sent = total.astype(BF16)

    def gather_late(g):
        a = pieces[g]
        if g % 2:
            pair = jnp.concatenate([a, exchange(a, 1)])
            return jnp.concatenate([pair, exchange(pair, 2)])
        b = exchange(a, 2)
        twin = exchange(jnp.concatenate([a, b]), 1)
        return jnp.concatenate([a, twin[:quarter], b, twin[quarter:]])

    low, top = inner_depth, depth - 1
    buckets = [zero] + [gather_late(g) for g in range(1, top) if g != low]
    chosen = jnp.where((place >> low & 1) == 1, pieces[low], pieces[top])
    got = {m: exchange(chosen, m) for m in (3, 2, 1)}
    full = jnp.concatenate([chosen, got[1], got[2], got[3]])
    buckets.append(full)
    buckets.append(exchange(full, 1 << low))
    return buckets


def per_device(queries, key_vectors, value_vectors, level_weights):
    inner_count = lax.axis_size("inner")
    inner_depth = inner_count.bit_length() - 1
    depth = inner_depth + lax.axis_size("outer").bit_length() - 1
    local_depth = queries.shape[0].bit_length() - 1
    place = lax.axis_index("outer") * inner_count + lax.axis_index("inner")
    where = place.astype(jnp.int32).reshape(1)
    far = lambda x: pltpu.with_memory_space_constraint(x, pltpu.HBM)
    queries, key_vectors, value_vectors = map(far, (queries, key_vectors, value_vectors))
    state, first = block_states(where, key_vectors, value_vectors)
    buckets = exchange_states(state, place, inner_depth, depth)
    above = local_depth + 1
    units = 2 * queries.shape[1] // HEAD_BLOCK
    given = (where, queries, key_vectors, value_vectors, level_weights, first)
    split = SPLIT * units // 4
    acc0, flat0 = local_part(0, split, *given)
    acc1, flat1 = local_part(split, units - split, *given)
    acc, flat = merge_part(
        where,
        (far(flat0), far(flat1)),
        (far(acc0), far(acc1)),
        level_weights,
        buckets[:2],
        ((above, 0), (above + 1, 1)),
    )
    return final_part(
        where, flat, acc, level_weights, buckets[2:], inner_depth, depth - 1
    )


def solution(mesh):
    placed = P(AXES, None, None)
    return jax.shard_map(
        per_device,
        mesh=mesh,
        in_specs=(placed, placed, placed, P(None, None, AXES)),
        out_specs=placed,
        check_vma=False,
    )
```

profile of v0, /device:TPU:0, one launch (start us, length us, event | category | flops | bytes accessed | tf_op | source)
XLA Modules:
  0.0 61.2 jit_solution(5637751329968081203)
XLA Ops:
  0.0 2.8 %states.1 = (bf16[16,128,128]{2,1,0:T(8,128)(2,1)S(1)}, bf16[16,128,128]{2,1,0:T(8,128)(2,1)S(1)}) custom-call(s32[1]{0:T(128)} %bitcast.place_ref, bf16[512,16,128]{2,1,0:T(8,128)(2,1)} %k_ref.5, bf16[512,16,128]{2,1,0:T(8,128)(2,1)} %v_ref.5), custom_call_target="tpu_custom_call" | custom-call | flops 268435456 | bytes 4194304 | tf_op jit(solution)/shard_map/states/pallas_call | solution.py:50
  2.8 0.0 copy-start
  2.9 3.0 %collective-permute-start = (bf16[4,128,128]{2,1,0:T(8,128)(2,1)S(1)}, bf16[4,128,128]{2,1,0:T(8,128)(2,1)S(1)}, u32[]{:S(2)}, u32[]{:S(2)}) collective-permute-start(bf16[4,128,128]{2,1,0:T(8,128)(2,1)S(1)} %get-tuple-element.33), channel_id=1, source_target_pairs={{0,1},{1,0},{2,3},{3,2},{4,5},{5,4},{6,7},{7,6},{8,9},{9,8},{10,11... | collective-permute-start | bytes 393224 | tf_op jit(solution)/shard_map/ppermute | solution.py:293
  5.9 1.5 %collective-permute-start.3 = (bf16[4,128,128]{2,1,0:T(8,128)(2,1)S(1)}, bf16[4,128,128]{2,1,0:T(8,128)(2,1)S(1)}, u32[]{:S(2)}, u32[]{:S(2)}) collective-permute-start(bf16[4,128,128]{2,1,0:T(8,128)(2,1)S(1)} %get-tuple-element.31), channel_id=1, source_target_pairs={{0,3},{1,2},{2,1},{3,0},{4,7},{5,6},{6,5},{7,4},{8,11},{9,10},{10,... | collective-permute-start | bytes 393224 | tf_op jit(solution)/shard_map/ppermute | solution.py:293
  7.4 0.0 collective-permute-start.2
  7.5 4.0 %collective-permute-done = bf16[4,128,128]{2,1,0:T(8,128)(2,1)S(1)} collective-permute-done((bf16[4,128,128]{2,1,0:T(8,128)(2,1)S(1)}, bf16[4,128,128]{2,1,0:T(8,128)(2,1)S(1)}, u32[]{:S(2)}, u32[]{:S(2)}) %collective-permute-start) | collective-permute-done | bytes 131104 | tf_op jit(solution)/shard_map/ppermute | solution.py:293
  11.5 1.7 %collective-permute-done.3 = bf16[4,128,128]{2,1,0:T(8,128)(2,1)S(1)} collective-permute-done((bf16[4,128,128]{2,1,0:T(8,128)(2,1)S(1)}, bf16[4,128,128]{2,1,0:T(8,128)(2,1)S(1)}, u32[]{:S(2)}, u32[]{:S(2)}) %collective-permute-start.3) | collective-permute-done | bytes 131104 | tf_op jit(solution)/shard_map/ppermute | solution.py:293
  13.2 0.4 collective-permute-done.2
  13.5 0.1 fusion.2
  13.6 2.8 %collective-permute-start.6 = (bf16[4,128,128]{2,1,0:T(8,128)(2,1)S(1)}, bf16[4,128,128]{2,1,0:T(8,128)(2,1)S(1)}, u32[]{:S(2)}, u32[]{:S(2)}) collective-permute-start(bf16[4,128,128]{2,1,0:T(8,128)(2,1)S(1)} %get-tuple-element.25), channel_id=1, source_target_pairs={{0,4},{1,5},{2,6},{3,7},{4,0},{5,1},{6,2},{7,3},{8,12},{9,13},{10,... | collective-permute-start | bytes 393224 | tf_op jit(solution)/shard_map/ppermute | solution.py:293
  16.5 5.4 %collective-permute-done.6 = bf16[4,128,128]{2,1,0:T(8,128)(2,1)S(1)} collective-permute-done((bf16[4,128,128]{2,1,0:T(8,128)(2,1)S(1)}, bf16[4,128,128]{2,1,0:T(8,128)(2,1)S(1)}, u32[]{:S(2)}, u32[]{:S(2)}) %collective-permute-start.6) | collective-permute-done | bytes 131104 | tf_op jit(solution)/shard_map/ppermute | solution.py:293
  21.9 0.1 collective-permute-start.9
  22.0 1.4 %collective-permute-start.1 = (bf16[12,128,128]{2,1,0:T(8,128)(2,1)S(1)}, bf16[12,128,128]{2,1,0:T(8,128)(2,1)S(1)}, u32[]{:S(2)}, u32[]{:S(2)}) collective-permute-start(bf16[12,128,128]{2,1,0:T(8,128)(2,1)S(1)} %pad_maximum_fusion.4), channel_id=1, source_target_pairs={{0,1},{1,0},{2,3},{3,2},{4,5},{5,4},{6,7},{7,6},{8,9},{9,8},{10,11... | collective-permute-start | bytes 1179656 | tf_op jit(solution)/shard_map/ppermute | solution.py:293
  23.4 0.0 copy-done
  23.4 3.3 %shard_map.47 = (f32[1,8,128,256]{3,2,1,0:T(8,128)}, bf16[1,8,256,128]{3,2,1,0:T(8,128)(2,1)}) custom-call(s32[1]{0:T(128)} %bitcast.place_ref, bf16[512,16,128]{2,1,0:T(8,128)(2,1)} %q_ref.3, bf16[512,16,128]{2,1,0:T(8,128)(2,1)} %k_ref.5, bf16[512,16,128]{2,1,0:T(8,128)(2,1)} %v_ref.5, f32[18,16,512]{2,1,0:T(8,128)S(1)} %copy-done, ...), custom_call_target="tpu_custom_call" | custom-call | flops 268435456 | bytes 3145728 | tf_op jit(solution)/shard_map/pallas_call | solution.py:134
  26.7 6.1 %shard_map.46 = (f32[3,8,128,256]{3,2,1,0:T(8,128)}, bf16[3,8,256,128]{3,2,1,0:T(8,128)(2,1)}) custom-call(s32[1]{0:T(128)} %bitcast.place_ref, bf16[512,16,128]{2,1,0:T(8,128)(2,1)} %q_ref.3, bf16[512,16,128]{2,1,0:T(8,128)(2,1)} %k_ref.5, bf16[512,16,128]{2,1,0:T(8,128)(2,1)} %v_ref.5, f32[18,16,512]{2,1,0:T(8,128)S(1)} %copy-done, ...), custom_call_target="tpu_custom_call" | custom-call | flops 805306368 | bytes 9437184 | tf_op jit(solution)/shard_map/pallas_call | solution.py:134
  32.8 0.7 %collective-permute-start.4 = (bf16[4,128,128]{2,1,0:T(8,128)(2,1)S(1)}, bf16[4,128,128]{2,1,0:T(8,128)(2,1)S(1)}, u32[]{:S(2)}, u32[]{:S(2)}) collective-permute-start(bf16[4,128,128]{2,1,0:T(8,128)(2,1)S(1)} %get-tuple-element.22), channel_id=1, source_target_pairs={{0,1},{1,0},{2,3},{3,2},{4,5},{5,4},{6,7},{7,6},{8,9},{9,8},{10,11... | collective-permute-start | bytes 393224 | tf_op jit(solution)/shard_map/ppermute | solution.py:293
  33.5 0.5 collective-permute-start.7
  34.0 0.0 collective-permute-done.9
  34.1 1.6 %collective-permute-start.10 = (bf16[4,128,128]{2,1,0:T(8,128)(2,1)S(1)}, bf16[4,128,128]{2,1,0:T(8,128)(2,1)S(1)}, u32[]{:S(2)}, u32[]{:S(2)}) collective-permute-start(bf16[4,128,128]{2,1,0:T(8,128)(2,1)S(1)} %add_convert_fusion), channel_id=1, source_target_pairs={{0,16},{1,17},{2,18},{3,19},{4,20},{5,21},{6,22},{7,23},{8,24},{9,... | collective-permute-start | bytes 393224 | tf_op jit(solution)/shard_map/ppermute | solution.py:293
  35.7 2.8 %collective-permute-done.4 = bf16[4,128,128]{2,1,0:T(8,128)(2,1)S(1)} collective-permute-done((bf16[4,128,128]{2,1,0:T(8,128)(2,1)S(1)}, bf16[4,128,128]{2,1,0:T(8,128)(2,1)S(1)}, u32[]{:S(2)}, u32[]{:S(2)}) %collective-permute-start.4) | collective-permute-done | bytes 131104 | tf_op jit(solution)/shard_map/ppermute | solution.py:293
  38.5 0.7 %collective-permute-start.5 = (bf16[8,128,128]{2,1,0:T(8,128)(2,1)S(1)}, bf16[8,128,128]{2,1,0:T(8,128)(2,1)S(1)}, u32[]{:S(2)}, u32[]{:S(2)}) collective-permute-start(bf16[8,128,128]{2,1,0:T(8,128)(2,1)S(1)} %pad_maximum_fusion.5), channel_id=1, source_target_pairs={{0,2},{1,3},{2,0},{3,1},{4,6},{5,7},{6,4},{7,5},{8,10},{9,11},{10,... | collective-permute-start | bytes 786440 | tf_op jit(solution)/shard_map/ppermute | solution.py:293
  39.2 0.0 collective-permute-done.7
  39.2 1.1 %collective-permute-start.8 = (bf16[8,128,128]{2,1,0:T(8,128)(2,1)S(1)}, bf16[8,128,128]{2,1,0:T(8,128)(2,1)S(1)}, u32[]{:S(2)}, u32[]{:S(2)}) collective-permute-start(bf16[8,128,128]{2,1,0:T(8,128)(2,1)S(1)} %pad_maximum_fusion.6), channel_id=1, source_target_pairs={{0,1},{1,0},{2,3},{3,2},{4,5},{5,4},{6,7},{7,6},{8,9},{9,8},{10,11... | collective-permute-start | bytes 786440 | tf_op jit(solution)/shard_map/ppermute | solution.py:293
  40.3 0.0 collective-permute-done.10
  40.3 1.9 %collective-permute-start.13 = (bf16[4,128,128]{2,1,0:T(8,128)(2,1)S(1)}, bf16[4,128,128]{2,1,0:T(8,128)(2,1)S(1)}, u32[]{:S(2)}, u32[]{:S(2)}) collective-permute-start(bf16[4,128,128]{2,1,0:T(8,128)(2,1)S(1)} %broadcast_select_fusion), channel_id=1, source_target_pairs={{0,3},{1,2},{2,1},{3,0},{4,7},{5,6},{6,5},{7,4},{8,11},{9,10},{10,... | collective-permute-start | bytes 393224 | tf_op jit(solution)/shard_map/ppermute | solution.py:293
  42.2 0.7 %collective-permute-start.12 = (bf16[4,128,128]{2,1,0:T(8,128)(2,1)S(1)}, bf16[4,128,128]{2,1,0:T(8,128)(2,1)S(1)}, u32[]{:S(2)}, u32[]{:S(2)}) collective-permute-start(bf16[4,128,128]{2,1,0:T(8,128)(2,1)S(1)} %broadcast_select_fusion), channel_id=1, source_target_pairs={{0,2},{1,3},{2,0},{3,1},{4,6},{5,7},{6,4},{7,5},{8,10},{9,11},{10,... | collective-permute-start | bytes 393224 | tf_op jit(solution)/shard_map/ppermute | solution.py:293
  42.9 0.0 collective-permute-done.1
  42.9 1.0 %collective-permute-start.11 = (bf16[4,128,128]{2,1,0:T(8,128)(2,1)S(1)}, bf16[4,128,128]{2,1,0:T(8,128)(2,1)S(1)}, u32[]{:S(2)}, u32[]{:S(2)}) collective-permute-start(bf16[4,128,128]{2,1,0:T(8,128)(2,1)S(1)} %broadcast_select_fusion), channel_id=1, source_target_pairs={{0,1},{1,0},{2,3},{3,2},{4,5},{5,4},{6,7},{7,6},{8,9},{9,8},{10,11... | collective-permute-start | bytes 393224 | tf_op jit(solution)/shard_map/ppermute | solution.py:293
  43.9 0.1 pad_maximum_fusion.rest_0_
  44.0 6.5 %collective-permute-done.13 = bf16[4,128,128]{2,1,0:T(8,128)(2,1)S(1)} collective-permute-done((bf16[4,128,128]{2,1,0:T(8,128)(2,1)S(1)}, bf16[4,128,128]{2,1,0:T(8,128)(2,1)S(1)}, u32[]{:S(2)}, u32[]{:S(2)}) %collective-permute-start.13) | collective-permute-done | bytes 131104 | tf_op jit(solution)/shard_map/ppermute | solution.py:293
  50.5 1.2 %collective-permute-done.12 = bf16[4,128,128]{2,1,0:T(8,128)(2,1)S(1)} collective-permute-done((bf16[4,128,128]{2,1,0:T(8,128)(2,1)S(1)}, bf16[4,128,128]{2,1,0:T(8,128)(2,1)S(1)}, u32[]{:S(2)}, u32[]{:S(2)}) %collective-permute-start.12) | collective-permute-done | bytes 131104 | tf_op jit(solution)/shard_map/ppermute | solution.py:293
  51.7 0.5 collective-permute-done.11
  52.2 0.1 pad_maximum_fusion.3.rest_1_
  52.3 0.1 collective-permute-start.14
  52.4 0.0 collective-permute-done.5
  52.4 0.1 pad_maximum_fusion.1.rest_1_
  52.4 4.9 %merge.1 = (f32[4,8,128,256]{3,2,1,0:T(8,128)S(1)}, bf16[4,8,256,128]{3,2,1,0:T(8,128)(2,1)S(1)}) custom-call(s32[1]{0:T(128)} %bitcast.place_ref, bf16[3,8,256,128]{3,2,1,0:T(8,128)(2,1)} %get-tuple-element.17.qa_ref, bf16[1,8,256,128]{3,2,1,0:T(8,128)(2,1)} %get-tuple-element.18.qb_ref, f32[3,8,128,256]{3,2,1,0:T(8,128)} %get-tuple-element.19.aa_ref, ...), custom_call_target="tpu_custom_call" | custom-call | flops 536870912 | bytes 12582912 | tf_op jit(solution)/shard_map/merge/pallas_call | solution.py:209
  57.3 0.0 collective-permute-done.8
  57.4 0.1 pad_maximum_fusion.2.rest_0_
  57.5 0.0 collective-permute-done.14.rest_2_
  57.5 3.7 %final.1 = bf16[512,16,128]{2,1,0:T(8,128)(2,1)} custom-call(s32[1]{0:T(128)} %bitcast.place_ref, bf16[4,8,256,128]{3,2,1,0:T(8,128)(2,1)S(1)} %get-tuple-element.23.q_ref, f32[4,8,128,256]{3,2,1,0:T(8,128)S(1)} %get-tuple-element.24.a_ref, f32[18,16,512]{2,1,0:T(8,128)S(1)} %copy-done, bf16[16,128,128]{2,1,0:T(8,128)(2,1)S(1)} %pad_maximum_fusion.2.rest_0_, ...), custom_call_target="tpu_custom_call" | custom-call | flops 805306368 | bytes 12582912 | tf_op jit(solution)/shard_map/final/pallas_call | solution.py:265
  (10 shorter events, 0.3 us)
Async XLA Ops:
  2.8 20.6 %copy-start = (f32[18,16,512]{2,1,0:T(8,128)S(1)}, f32[18,16,512]{2,1,0:T(8,128)}, u32[]{:S(2)}) copy-start(f32[18,16,512]{2,1,0:T(8,128)} %w_ref.7) | copy-start | bytes 1769476
  2.9 8.6 %collective-permute-start = (bf16[4,128,128]{2,1,0:T(8,128)(2,1)S(1)}, bf16[4,128,128]{2,1,0:T(8,128)(2,1)S(1)}, u32[]{:S(2)}, u32[]{:S(2)}) collective-permute-start(bf16[4,128,128]{2,1,0:T(8,128)(2,1)S(1)} %get-tuple-element.33), channel_id=1, source_target_pairs={{0,1},{1,0},{2,3},{3,2},{4,5},{5,4},{6,7},{7,6},{8,9},{9,8},{10,11... | collective-permute-start | bytes 393224 | tf_op jit(solution)/shard_map/ppermute | solution.py:293
  5.9 7.3 %collective-permute-start.3 = (bf16[4,128,128]{2,1,0:T(8,128)(2,1)S(1)}, bf16[4,128,128]{2,1,0:T(8,128)(2,1)S(1)}, u32[]{:S(2)}, u32[]{:S(2)}) collective-permute-start(bf16[4,128,128]{2,1,0:T(8,128)(2,1)S(1)} %get-tuple-element.31), channel_id=1, source_target_pairs={{0,3},{1,2},{2,1},{3,0},{4,7},{5,6},{6,5},{7,4},{8,11},{9,10},{10,... | collective-permute-start | bytes 393224 | tf_op jit(solution)/shard_map/ppermute | solution.py:293
  7.4 6.1 %collective-permute-start.2 = (bf16[4,128,128]{2,1,0:T(8,128)(2,1)S(1)}, bf16[4,128,128]{2,1,0:T(8,128)(2,1)S(1)}, u32[]{:S(2)}, u32[]{:S(2)}) collective-permute-start(bf16[4,128,128]{2,1,0:T(8,128)(2,1)S(1)} %get-tuple-element.30), channel_id=1, source_target_pairs={{0,2},{1,3},{2,0},{3,1},{4,6},{5,7},{6,4},{7,5},{8,10},{9,11},{10,... | collective-permute-start | bytes 393224 | tf_op jit(solution)/shard_map/ppermute | solution.py:293
  13.6 8.2 %collective-permute-start.6 = (bf16[4,128,128]{2,1,0:T(8,128)(2,1)S(1)}, bf16[4,128,128]{2,1,0:T(8,128)(2,1)S(1)}, u32[]{:S(2)}, u32[]{:S(2)}) collective-permute-start(bf16[4,128,128]{2,1,0:T(8,128)(2,1)S(1)} %get-tuple-element.25), channel_id=1, source_target_pairs={{0,4},{1,5},{2,6},{3,7},{4,0},{5,1},{6,2},{7,3},{8,12},{9,13},{10,... | collective-permute-start | bytes 393224 | tf_op jit(solution)/shard_map/ppermute | solution.py:293
  21.9 12.2 %collective-permute-start.9 = (bf16[4,128,128]{2,1,0:T(8,128)(2,1)S(1)}, bf16[4,128,128]{2,1,0:T(8,128)(2,1)S(1)}, u32[]{:S(2)}, u32[]{:S(2)}) collective-permute-start(bf16[4,128,128]{2,1,0:T(8,128)(2,1)S(1)} %fusion.1), channel_id=1, source_target_pairs={{0,8},{1,9},{2,10},{3,11},{4,12},{5,13},{6,14},{7,15},{8,0},{9,1},... | collective-permute-start | bytes 393224 | tf_op jit(solution)/shard_map/ppermute | solution.py:293
  22.0 20.9 %collective-permute-start.1 = (bf16[12,128,128]{2,1,0:T(8,128)(2,1)S(1)}, bf16[12,128,128]{2,1,0:T(8,128)(2,1)S(1)}, u32[]{:S(2)}, u32[]{:S(2)}) collective-permute-start(bf16[12,128,128]{2,1,0:T(8,128)(2,1)S(1)} %pad_maximum_fusion.4), channel_id=1, source_target_pairs={{0,1},{1,0},{2,3},{3,2},{4,5},{5,4},{6,7},{7,6},{8,9},{9,8},{10,11... | collective-permute-start | bytes 1179656 | tf_op jit(solution)/shard_map/ppermute | solution.py:293
  32.8 5.6 %collective-permute-start.4 = (bf16[4,128,128]{2,1,0:T(8,128)(2,1)S(1)}, bf16[4,128,128]{2,1,0:T(8,128)(2,1)S(1)}, u32[]{:S(2)}, u32[]{:S(2)}) collective-permute-start(bf16[4,128,128]{2,1,0:T(8,128)(2,1)S(1)} %get-tuple-element.22), channel_id=1, source_target_pairs={{0,1},{1,0},{2,3},{3,2},{4,5},{5,4},{6,7},{7,6},{8,9},{9,8},{10,11... | collective-permute-start | bytes 393224 | tf_op jit(solution)/shard_map/ppermute | solution.py:293
  33.5 5.7 %collective-permute-start.7 = (bf16[4,128,128]{2,1,0:T(8,128)(2,1)S(1)}, bf16[4,128,128]{2,1,0:T(8,128)(2,1)S(1)}, u32[]{:S(2)}, u32[]{:S(2)}) collective-permute-start(bf16[4,128,128]{2,1,0:T(8,128)(2,1)S(1)} %collective-permute-done.6), channel_id=1, source_target_pairs={{0,2},{1,3},{2,0},{3,1},{4,6},{5,7},{6,4},{7,5},{8,10},{9,11},{10,... | collective-permute-start | bytes 393224 | tf_op jit(solution)/shard_map/ppermute | solution.py:293
  34.1 6.2 %collective-permute-start.10 = (bf16[4,128,128]{2,1,0:T(8,128)(2,1)S(1)}, bf16[4,128,128]{2,1,0:T(8,128)(2,1)S(1)}, u32[]{:S(2)}, u32[]{:S(2)}) collective-permute-start(bf16[4,128,128]{2,1,0:T(8,128)(2,1)S(1)} %add_convert_fusion), channel_id=1, source_target_pairs={{0,16},{1,17},{2,18},{3,19},{4,20},{5,21},{6,22},{7,23},{8,24},{9,... | collective-permute-start | bytes 393224 | tf_op jit(solution)/shard_map/ppermute | solution.py:293
  38.5 13.9 %collective-permute-start.5 = (bf16[8,128,128]{2,1,0:T(8,128)(2,1)S(1)}, bf16[8,128,128]{2,1,0:T(8,128)(2,1)S(1)}, u32[]{:S(2)}, u32[]{:S(2)}) collective-permute-start(bf16[8,128,128]{2,1,0:T(8,128)(2,1)S(1)} %pad_maximum_fusion.5), channel_id=1, source_target_pairs={{0,2},{1,3},{2,0},{3,1},{4,6},{5,7},{6,4},{7,5},{8,10},{9,11},{10,... | collective-permute-start | bytes 786440 | tf_op jit(solution)/shard_map/ppermute | solution.py:293
  39.2 18.1 %collective-permute-start.8 = (bf16[8,128,128]{2,1,0:T(8,128)(2,1)S(1)}, bf16[8,128,128]{2,1,0:T(8,128)(2,1)S(1)}, u32[]{:S(2)}, u32[]{:S(2)}) collective-permute-start(bf16[8,128,128]{2,1,0:T(8,128)(2,1)S(1)} %pad_maximum_fusion.6), channel_id=1, source_target_pairs={{0,1},{1,0},{2,3},{3,2},{4,5},{5,4},{6,7},{7,6},{8,9},{9,8},{10,11... | collective-permute-start | bytes 786440 | tf_op jit(solution)/shard_map/ppermute | solution.py:293
  40.3 10.2 %collective-permute-start.13 = (bf16[4,128,128]{2,1,0:T(8,128)(2,1)S(1)}, bf16[4,128,128]{2,1,0:T(8,128)(2,1)S(1)}, u32[]{:S(2)}, u32[]{:S(2)}) collective-permute-start(bf16[4,128,128]{2,1,0:T(8,128)(2,1)S(1)} %broadcast_select_fusion), channel_id=1, source_target_pairs={{0,3},{1,2},{2,1},{3,0},{4,7},{5,6},{6,5},{7,4},{8,11},{9,10},{10,... | collective-permute-start | bytes 393224 | tf_op jit(solution)/shard_map/ppermute | solution.py:293
  42.2 9.5 %collective-permute-start.12 = (bf16[4,128,128]{2,1,0:T(8,128)(2,1)S(1)}, bf16[4,128,128]{2,1,0:T(8,128)(2,1)S(1)}, u32[]{:S(2)}, u32[]{:S(2)}) collective-permute-start(bf16[4,128,128]{2,1,0:T(8,128)(2,1)S(1)} %broadcast_select_fusion), channel_id=1, source_target_pairs={{0,2},{1,3},{2,0},{3,1},{4,6},{5,7},{6,4},{7,5},{8,10},{9,11},{10,... | collective-permute-start | bytes 393224 | tf_op jit(solution)/shard_map/ppermute | solution.py:293
  42.9 9.3 %collective-permute-start.11 = (bf16[4,128,128]{2,1,0:T(8,128)(2,1)S(1)}, bf16[4,128,128]{2,1,0:T(8,128)(2,1)S(1)}, u32[]{:S(2)}, u32[]{:S(2)}) collective-permute-start(bf16[4,128,128]{2,1,0:T(8,128)(2,1)S(1)} %broadcast_select_fusion), channel_id=1, source_target_pairs={{0,1},{1,0},{2,3},{3,2},{4,5},{5,4},{6,7},{7,6},{8,9},{9,8},{10,11... | collective-permute-start | bytes 393224 | tf_op jit(solution)/shard_map/ppermute | solution.py:293
  52.3 5.2 %collective-permute-start.14 = (bf16[16,128,128]{2,1,0:T(8,128)(2,1)S(1)}, bf16[16,128,128]{2,1,0:T(8,128)(2,1)S(1)}, u32[]{:S(2)}, u32[]{:S(2)}) collective-permute-start(bf16[16,128,128]{2,1,0:T(8,128)(2,1)S(1)} %pad_maximum_fusion.3.rest_1_), channel_id=1, source_target_pairs={{0,8},{1,9},{2,10},{3,11},{4,12},{5,13},{6,14},{7,15},{8,0},{9,1},... | collective-permute-start | bytes 1572872 | tf_op jit(solution)/shard_map/ppermute | solution.py:293
where the time goes:
time: 61.4 us; the launch traced here: 61.2 us
  waiting for transfers between devices  22.5 us (37%)
  Pallas kernels  20.9 us (34%)
  starting transfers between devices  17.1 us (28%)
    ppermute x15, waiting for transfers between devices, exchange(): return lax.ppermute(value, AXES, pairs)  22.5 us
    ppermute x15, starting transfers between devices, exchange(): return lax.ppermute(value, AXES, pairs)  17.1 us
    pallas_call x2, Pallas kernels, local_part(): pl.pallas_call(functools.partial(local_kernel, start, blocks), grid_spec=...  9.42 us
    pallas_call x1, Pallas kernels, merge_part(): pl.pallas_call(functools.partial(merge_kernel, levels, blocks, split), gr...  4.9 us
    pallas_call x1, Pallas kernels, final_part(): pl.pallas_call(functools.partial(final_kernel, ((2 * tile).bit_length(),...  3.74 us
    pallas_call x1, Pallas kernels, block_states(): pl.pallas_call(state_kernel, grid_spec=scalar_grid((2,), [source, source]...  2.79 us
  transfers between devices with their start and end apart: 15, of which 8 were waited for; matrix products, arithmetic and copies ran while one was open for 1% of the time, Pallas kernels for 23%

commit v1 on v0

--- a/solution.py
+++ b/solution.py
@@ -182,32 +182,42 @@
     return total
 
 
-def merge_kernel(levels, blocks, split, place_ref, qa_ref, qb_ref, aa_ref, ab_ref, w_ref, *rest):
-    refs, (acc_ref, qh_ref) = rest[:-2], rest[-2:]
-    rows = [gain_row(place_ref[0], *level) for level in levels]
+def merge_kernel(levels, late, blocks, split, place_ref, qa_ref, qb_ref, aa_ref, ab_ref, w_ref, *rest):
+    refs, (acc_ref, scaled_ref) = rest[:-2], rest[-2:]
+    place = place_ref[0]
+    rows = [gain_row(place, *level) for level in levels]
+    above, low, top = late
+    bit = lambda g: (place >> g & 1).astype(F32)
+    level = lambda g, c: (above + g, c * 2.0 ** (-0.5 * (above + g)))
+    tail = [gain_row(place, above + g, g) for g in range(2, top) if g != low]
+    tail.append([level(low, bit(low)), level(top, bit(top) * (1.0 - bit(low)))])
+    tail.append([level(top, bit(top) * bit(low))])
     unit = pl.program_id(0)
 
     def take(q_ref, a_ref):
-        qh_ref[...] = q_ref[...]
+        dim = q_ref.shape[2]
         for h in range(q_ref.shape[0]):
-            acc_ref[h] = a_ref[h] + bucket_sum(
-                place_ref[0], unit % blocks, w_ref, q_ref, h, refs, rows
+            acc_ref[unit, h] = a_ref[h] + bucket_sum(
+                place, unit % blocks, w_ref, q_ref, h, refs, rows
             )
+            turned = q_ref[h].T.astype(F32)
+            for n, row in enumerate(tail):
+                gain = sum(w_ref[l, h : h + 1, :] * c for l, c in row)
+                scaled_ref[unit, h, n * dim : (n + 1) * dim, :] = (turned * gain).astype(BF16)
 
     pl.when(unit < split)(lambda: take(qa_ref, aa_ref))
     pl.when(unit >= split)(lambda: take(qb_ref, ab_ref))
 
 
-def merge_part(place, turned, accs, level_weights, buckets, levels):
+def merge_part(place, turned, accs, level_weights, buckets, levels, late, count):
     split, block, tile, dim = turned[0].shape
     units = split + turned[1].shape[0]
     blocks = units // 2
-    heads = block * blocks
     ahead = lambda i, p: (jnp.minimum(i, split - 1), 0, 0, 0)
     after = lambda i, p: (jnp.maximum(i - split, 0), 0, 0, 0)
-    each = lambda i, p: (i, 0, 0, 0)
+    whole = pl.BlockSpec(memory_space=pltpu.VMEM)
     return pl.pallas_call(
-        functools.partial(merge_kernel, levels, blocks, split),
+        functools.partial(merge_kernel, levels, late, blocks, split),
         grid_spec=scalar_grid(
             (units,),
             [
@@ -219,15 +229,12 @@
                     (level_weights.shape[0], block, tile), lambda i, p: (0, i % blocks, i // blocks)
                 ),
             ]
-            + [pl.BlockSpec((heads, dim, dim), lambda i, p: (0, 0, 0))] * len(buckets),
-            [
-                pl.BlockSpec((None, block, dim, tile), each),
-                pl.BlockSpec((None, block, tile, dim), each),
-            ],
+            + [whole] * len(buckets),
+            [whole, whole],
         ),
         out_shape=[
             MERGE_SPACE((units, block, dim, tile), F32),
-            MERGE_SPACE((units, block, tile, dim), BF16),
+            MERGE_SPACE((units, block, count * dim, tile), BF16),
         ],
         name="merge",
         compiler_params=pltpu.CompilerParams(vmem_limit_bytes=MERGE_VMEM),
@@ -239,41 +246,31 @@
     )(place, *turned, *accs, level_weights, *buckets)
 
 
-def final_kernel(meta, place_ref, q_ref, a_ref, w_ref, *rest):
+def final_kernel(blocks, place_ref, scaled_ref, a_ref, *rest):
     refs, out_ref = rest[:-1], rest[-1]
-    above, low, top, blocks = meta
-    place = place_ref[0]
-    bit = lambda g: (place >> g & 1).astype(F32)
-    level = lambda g, c: (above + g, c * 2.0 ** (-0.5 * (above + g)))
-    rows = [gain_row(place, above + g, g) for g in range(2, top) if g != low]
-    rows.append([level(low, bit(low)), level(top, bit(top) * (1.0 - bit(low)))])
-    rows.append([level(top, bit(top) * bit(low))])
+    unit = pl.program_id(0)
+    block = scaled_ref.shape[1]
+    quarter = refs[0].shape[0] // 4
     done = []
-    for h in range(q_ref.shape[0]):
-        total = a_ref[h] + bucket_sum(
-            place, pl.program_id(0) % blocks, w_ref, q_ref, h, refs, rows
-        )
+    for h in range(block):
+        spot = unit % blocks * block + h
+        spot = (spot // quarter ^ (place_ref[0] & 3)) * quarter + spot % quarter
+        wide = jnp.concatenate([ref[spot] for ref in refs], axis=1)
+        total = a_ref[unit, h] + jnp.dot(wide, scaled_ref[unit, h], preferred_element_type=F32)
         done.append(total.T.astype(BF16))
     out_ref[...] = jnp.swapaxes(jnp.stack(done), 0, 1)
 
 
-def final_part(place, turned, acc, level_weights, buckets, low, top):
-    units, block, tile, dim = turned.shape
+def final_part(place, scaled, acc, buckets):
+    units, block, dim, tile = acc.shape
     blocks = units // 2
     heads = block * blocks
-    each = lambda i, p: (i, 0, 0, 0)
+    whole = pl.BlockSpec(memory_space=pltpu.VMEM)
     return pl.pallas_call(
-        functools.partial(final_kernel, ((2 * tile).bit_length(), low, top, blocks)),
+        functools.partial(final_kernel, blocks),
         grid_spec=scalar_grid(
             (units,),
-            [
-                pl.BlockSpec((None, block, tile, dim), each),
-                pl.BlockSpec((None, block, dim, tile), each),
-                pl.BlockSpec(
-                    (level_weights.shape[0], block, tile), lambda i, p: (0, i % blocks, i // blocks)
-                ),
-            ]
-            + [pl.BlockSpec((heads, dim, dim), lambda i, p: (0, 0, 0))] * len(buckets),
+            [whole, whole] + [whole] * len(buckets),
             pl.BlockSpec((tile, block, dim), lambda i, p: (i // blocks, i % blocks, 0)),
         ),
         out_shape=jax.ShapeDtypeStruct((2 * tile, heads, dim), BF16),
@@ -284,7 +281,7 @@
             bytes_accessed=12 * units * block * tile * dim,
             transcendentals=0,
         ),
-    )(place, turned, acc, level_weights, *buckets)
+    )(place, scaled, acc, *buckets)
 
 
 def exchange(value, mask):
@@ -347,17 +344,17 @@
     split = SPLIT * units // 4
     acc0, flat0 = local_part(0, split, *given)
     acc1, flat1 = local_part(split, units - split, *given)
-    acc, flat = merge_part(
+    acc, scaled = merge_part(
         where,
         (far(flat0), far(flat1)),
         (far(acc0), far(acc1)),
         level_weights,
         buckets[:2],
         ((above, 0), (above + 1, 1)),
+        (above, inner_depth, depth - 1),
+        len(buckets) - 2,
     )
-    return final_part(
-        where, flat, acc, level_weights, buckets[2:], inner_depth, depth - 1
-    )
+    return final_part(where, scaled, acc, buckets[2:])
 
 
 def solution(mesh):

time: 61.4 us -> 61.2 us (level)
  transfers between devices with their start and end apart: 15 -> 15, of which waited for: 8 -> 8; matrix products, arithmetic and copies ran while one was open for 1% -> 1% of each run, Pallas kernels for 23% -> 24%
where the time goes in v1:
time: 61.2 us; the launch traced here: 61 us
  waiting for transfers between devices  22.5 us (37%)
  Pallas kernels  20.6 us (34%)
  starting transfers between devices  17.1 us (28%)
    ppermute x15, waiting for transfers between devices, exchange(): return lax.ppermute(value, AXES, pairs)  22.5 us
    ppermute x15, starting transfers between devices, exchange(): return lax.ppermute(value, AXES, pairs)  17.1 us
    pallas_call x2, Pallas kernels, local_part(): pl.pallas_call(functools.partial(local_kernel, start, blocks), grid_spec=...  9.42 us
    pallas_call x1, Pallas kernels, merge_part(): pl.pallas_call(functools.partial(merge_kernel, levels, late, blocks, spli...  5.19 us
    pallas_call x1, Pallas kernels, final_part(): pl.pallas_call(functools.partial(final_kernel, blocks), grid_spec=scalar_...  3.21 us
    pallas_call x1, Pallas kernels, block_states(): pl.pallas_call(state_kernel, grid_spec=scalar_grid((2,), [source, source]...  2.79 us
  transfers between devices with their start and end apart: 15, of which 8 were waited for; matrix products, arithmetic and copies ran while one was open for 1% of the time, Pallas kernels for 24%

profile of v1, /device:TPU:0, one launch (start us, length us, event | category | flops | bytes accessed | tf_op | source)
XLA Modules:
  0.0 61.0 jit_solution(15639580455275233083)
XLA Ops:
  0.0 2.8 %states.1 = (bf16[16,128,128]{2,1,0:T(8,128)(2,1)S(1)}, bf16[16,128,128]{2,1,0:T(8,128)(2,1)S(1)}) custom-call(s32[1]{0:T(128)} %bitcast.place_ref, bf16[512,16,128]{2,1,0:T(8,128)(2,1)} %k_ref.5, bf16[512,16,128]{2,1,0:T(8,128)(2,1)} %v_ref.5), custom_call_target="tpu_custom_call" | custom-call | flops 268435456 | bytes 4194304 | tf_op jit(solution)/shard_map/states/pallas_call | solution.py:50
  2.8 0.0 copy-start
  2.9 3.0 %collective-permute-start = (bf16[4,128,128]{2,1,0:T(8,128)(2,1)S(1)}, bf16[4,128,128]{2,1,0:T(8,128)(2,1)S(1)}, u32[]{:S(2)}, u32[]{:S(2)}) collective-permute-start(bf16[4,128,128]{2,1,0:T(8,128)(2,1)S(1)} %get-tuple-element.33), channel_id=1, source_target_pairs={{0,1},{1,0},{2,3},{3,2},{4,5},{5,4},{6,7},{7,6},{8,9},{9,8},{10,11... | collective-permute-start | bytes 393224 | tf_op jit(solution)/shard_map/ppermute | solution.py:290
  5.9 1.5 %collective-permute-start.3 = (bf16[4,128,128]{2,1,0:T(8,128)(2,1)S(1)}, bf16[4,128,128]{2,1,0:T(8,128)(2,1)S(1)}, u32[]{:S(2)}, u32[]{:S(2)}) collective-permute-start(bf16[4,128,128]{2,1,0:T(8,128)(2,1)S(1)} %get-tuple-element.31), channel_id=1, source_target_pairs={{0,3},{1,2},{2,1},{3,0},{4,7},{5,6},{6,5},{7,4},{8,11},{9,10},{10,... | collective-permute-start | bytes 393224 | tf_op jit(solution)/shard_map/ppermute | solution.py:290
  7.4 0.0 collective-permute-start.2
  7.5 4.0 %collective-permute-done = bf16[4,128,128]{2,1,0:T(8,128)(2,1)S(1)} collective-permute-done((bf16[4,128,128]{2,1,0:T(8,128)(2,1)S(1)}, bf16[4,128,128]{2,1,0:T(8,128)(2,1)S(1)}, u32[]{:S(2)}, u32[]{:S(2)}) %collective-permute-start) | collective-permute-done | bytes 131104 | tf_op jit(solution)/shard_map/ppermute | solution.py:290
  11.5 1.7 %collective-permute-done.3 = bf16[4,128,128]{2,1,0:T(8,128)(2,1)S(1)} collective-permute-done((bf16[4,128,128]{2,1,0:T(8,128)(2,1)S(1)}, bf16[4,128,128]{2,1,0:T(8,128)(2,1)S(1)}, u32[]{:S(2)}, u32[]{:S(2)}) %collective-permute-start.3) | collective-permute-done | bytes 131104 | tf_op jit(solution)/shard_map/ppermute | solution.py:290
  13.2 0.4 collective-permute-done.2
  13.5 0.1 fusion.2
  13.6 2.8 %collective-permute-start.6 = (bf16[4,128,128]{2,1,0:T(8,128)(2,1)S(1)}, bf16[4,128,128]{2,1,0:T(8,128)(2,1)S(1)}, u32[]{:S(2)}, u32[]{:S(2)}) collective-permute-start(bf16[4,128,128]{2,1,0:T(8,128)(2,1)S(1)} %get-tuple-element.25), channel_id=1, source_target_pairs={{0,4},{1,5},{2,6},{3,7},{4,0},{5,1},{6,2},{7,3},{8,12},{9,13},{10,... | collective-permute-start | bytes 393224 | tf_op jit(solution)/shard_map/ppermute | solution.py:290
  16.5 5.4 %collective-permute-done.6 = bf16[4,128,128]{2,1,0:T(8,128)(2,1)S(1)} collective-permute-done((bf16[4,128,128]{2,1,0:T(8,128)(2,1)S(1)}, bf16[4,128,128]{2,1,0:T(8,128)(2,1)S(1)}, u32[]{:S(2)}, u32[]{:S(2)}) %collective-permute-start.6) | collective-permute-done | bytes 131104 | tf_op jit(solution)/shard_map/ppermute | solution.py:290
  21.9 0.1 collective-permute-start.9
  22.0 1.4 %collective-permute-start.1 = (bf16[12,128,128]{2,1,0:T(8,128)(2,1)S(1)}, bf16[12,128,128]{2,1,0:T(8,128)(2,1)S(1)}, u32[]{:S(2)}, u32[]{:S(2)}) collective-permute-start(bf16[12,128,128]{2,1,0:T(8,128)(2,1)S(1)} %pad_maximum_fusion.4), channel_id=1, source_target_pairs={{0,1},{1,0},{2,3},{3,2},{4,5},{5,4},{6,7},{7,6},{8,9},{9,8},{10,11... | collective-permute-start | bytes 1179656 | tf_op jit(solution)/shard_map/ppermute | solution.py:290
  23.4 0.0 copy-done
  23.4 3.3 %shard_map.47 = (f32[1,8,128,256]{3,2,1,0:T(8,128)}, bf16[1,8,256,128]{3,2,1,0:T(8,128)(2,1)}) custom-call(s32[1]{0:T(128)} %bitcast.place_ref, bf16[512,16,128]{2,1,0:T(8,128)(2,1)} %q_ref.3, bf16[512,16,128]{2,1,0:T(8,128)(2,1)} %k_ref.5, bf16[512,16,128]{2,1,0:T(8,128)(2,1)} %v_ref.5, f32[18,16,512]{2,1,0:T(8,128)S(1)} %copy-done, ...), custom_call_target="tpu_custom_call" | custom-call | flops 268435456 | bytes 3145728 | tf_op jit(solution)/shard_map/pallas_call | solution.py:134
  26.7 6.1 %shard_map.46 = (f32[3,8,128,256]{3,2,1,0:T(8,128)}, bf16[3,8,256,128]{3,2,1,0:T(8,128)(2,1)}) custom-call(s32[1]{0:T(128)} %bitcast.place_ref, bf16[512,16,128]{2,1,0:T(8,128)(2,1)} %q_ref.3, bf16[512,16,128]{2,1,0:T(8,128)(2,1)} %k_ref.5, bf16[512,16,128]{2,1,0:T(8,128)(2,1)} %v_ref.5, f32[18,16,512]{2,1,0:T(8,128)S(1)} %copy-done, ...), custom_call_target="tpu_custom_call" | custom-call | flops 805306368 | bytes 9437184 | tf_op jit(solution)/shard_map/pallas_call | solution.py:134
  32.8 0.7 %collective-permute-start.4 = (bf16[4,128,128]{2,1,0:T(8,128)(2,1)S(1)}, bf16[4,128,128]{2,1,0:T(8,128)(2,1)S(1)}, u32[]{:S(2)}, u32[]{:S(2)}) collective-permute-start(bf16[4,128,128]{2,1,0:T(8,128)(2,1)S(1)} %get-tuple-element.22), channel_id=1, source_target_pairs={{0,1},{1,0},{2,3},{3,2},{4,5},{5,4},{6,7},{7,6},{8,9},{9,8},{10,11... | collective-permute-start | bytes 393224 | tf_op jit(solution)/shard_map/ppermute | solution.py:290
  33.5 0.5 collective-permute-start.7
  34.0 0.0 collective-permute-done.9
  34.1 1.6 %collective-permute-start.10 = (bf16[4,128,128]{2,1,0:T(8,128)(2,1)S(1)}, bf16[4,128,128]{2,1,0:T(8,128)(2,1)S(1)}, u32[]{:S(2)}, u32[]{:S(2)}) collective-permute-start(bf16[4,128,128]{2,1,0:T(8,128)(2,1)S(1)} %add_convert_fusion), channel_id=1, source_target_pairs={{0,16},{1,17},{2,18},{3,19},{4,20},{5,21},{6,22},{7,23},{8,24},{9,... | collective-permute-start | bytes 393224 | tf_op jit(solution)/shard_map/ppermute | solution.py:290
  35.7 2.8 %collective-permute-done.4 = bf16[4,128,128]{2,1,0:T(8,128)(2,1)S(1)} collective-permute-done((bf16[4,128,128]{2,1,0:T(8,128)(2,1)S(1)}, bf16[4,128,128]{2,1,0:T(8,128)(2,1)S(1)}, u32[]{:S(2)}, u32[]{:S(2)}) %collective-permute-start.4) | collective-permute-done | bytes 131104 | tf_op jit(solution)/shard_map/ppermute | solution.py:290
  38.5 0.7 %collective-permute-start.5 = (bf16[8,128,128]{2,1,0:T(8,128)(2,1)S(1)}, bf16[8,128,128]{2,1,0:T(8,128)(2,1)S(1)}, u32[]{:S(2)}, u32[]{:S(2)}) collective-permute-start(bf16[8,128,128]{2,1,0:T(8,128)(2,1)S(1)} %pad_maximum_fusion.5), channel_id=1, source_target_pairs={{0,2},{1,3},{2,0},{3,1},{4,6},{5,7},{6,4},{7,5},{8,10},{9,11},{10,... | collective-permute-start | bytes 786440 | tf_op jit(solution)/shard_map/ppermute | solution.py:290
  39.2 0.0 collective-permute-done.7
  39.2 1.1 %collective-permute-start.8 = (bf16[8,128,128]{2,1,0:T(8,128)(2,1)S(1)}, bf16[8,128,128]{2,1,0:T(8,128)(2,1)S(1)}, u32[]{:S(2)}, u32[]{:S(2)}) collective-permute-start(bf16[8,128,128]{2,1,0:T(8,128)(2,1)S(1)} %pad_maximum_fusion.6), channel_id=1, source_target_pairs={{0,1},{1,0},{2,3},{3,2},{4,5},{5,4},{6,7},{7,6},{8,9},{9,8},{10,11... | collective-permute-start | bytes 786440 | tf_op jit(solution)/shard_map/ppermute | solution.py:290
  40.3 0.0 collective-permute-done.10
  40.3 1.9 %collective-permute-start.13 = (bf16[4,128,128]{2,1,0:T(8,128)(2,1)S(1)}, bf16[4,128,128]{2,1,0:T(8,128)(2,1)S(1)}, u32[]{:S(2)}, u32[]{:S(2)}) collective-permute-start(bf16[4,128,128]{2,1,0:T(8,128)(2,1)S(1)} %broadcast_select_fusion), channel_id=1, source_target_pairs={{0,3},{1,2},{2,1},{3,0},{4,7},{5,6},{6,5},{7,4},{8,11},{9,10},{10,... | collective-permute-start | bytes 393224 | tf_op jit(solution)/shard_map/ppermute | solution.py:290
  42.2 0.7 %collective-permute-start.12 = (bf16[4,128,128]{2,1,0:T(8,128)(2,1)S(1)}, bf16[4,128,128]{2,1,0:T(8,128)(2,1)S(1)}, u32[]{:S(2)}, u32[]{:S(2)}) collective-permute-start(bf16[4,128,128]{2,1,0:T(8,128)(2,1)S(1)} %broadcast_select_fusion), channel_id=1, source_target_pairs={{0,2},{1,3},{2,0},{3,1},{4,6},{5,7},{6,4},{7,5},{8,10},{9,11},{10,... | collective-permute-start | bytes 393224 | tf_op jit(solution)/shard_map/ppermute | solution.py:290
  42.9 0.0 collective-permute-done.1
  42.9 1.0 %collective-permute-start.11 = (bf16[4,128,128]{2,1,0:T(8,128)(2,1)S(1)}, bf16[4,128,128]{2,1,0:T(8,128)(2,1)S(1)}, u32[]{:S(2)}, u32[]{:S(2)}) collective-permute-start(bf16[4,128,128]{2,1,0:T(8,128)(2,1)S(1)} %broadcast_select_fusion), channel_id=1, source_target_pairs={{0,1},{1,0},{2,3},{3,2},{4,5},{5,4},{6,7},{7,6},{8,9},{9,8},{10,11... | collective-permute-start | bytes 393224 | tf_op jit(solution)/shard_map/ppermute | solution.py:290
  43.9 0.1 pad_maximum_fusion.rest_0_
  44.0 6.5 %collective-permute-done.13 = bf16[4,128,128]{2,1,0:T(8,128)(2,1)S(1)} collective-permute-done((bf16[4,128,128]{2,1,0:T(8,128)(2,1)S(1)}, bf16[4,128,128]{2,1,0:T(8,128)(2,1)S(1)}, u32[]{:S(2)}, u32[]{:S(2)}) %collective-permute-start.13) | collective-permute-done | bytes 131104 | tf_op jit(solution)/shard_map/ppermute | solution.py:290
  50.5 1.2 %collective-permute-done.12 = bf16[4,128,128]{2,1,0:T(8,128)(2,1)S(1)} collective-permute-done((bf16[4,128,128]{2,1,0:T(8,128)(2,1)S(1)}, bf16[4,128,128]{2,1,0:T(8,128)(2,1)S(1)}, u32[]{:S(2)}, u32[]{:S(2)}) %collective-permute-start.12) | collective-permute-done | bytes 131104 | tf_op jit(solution)/shard_map/ppermute | solution.py:290
  51.7 0.5 collective-permute-done.11
  52.2 0.1 pad_maximum_fusion.3.rest_1_
  52.3 0.1 collective-permute-start.14
  52.4 0.0 collective-permute-done.5
  52.4 0.1 pad_maximum_fusion.1.rest_1_
  52.4 5.2 %merge.1 = (f32[4,8,128,256]{3,2,1,0:T(8,128)S(1)}, bf16[4,8,384,256]{3,2,1,0:T(8,128)(2,1)S(1)}) custom-call(s32[1]{0:T(128)} %bitcast.place_ref, bf16[3,8,256,128]{3,2,1,0:T(8,128)(2,1)} %get-tuple-element.17.qa_ref, bf16[1,8,256,128]{3,2,1,0:T(8,128)(2,1)} %get-tuple-element.18.qb_ref, f32[3,8,128,256]{3,2,1,0:T(8,128)} %get-tuple-element.19.aa_ref, ...), custom_call_target="tpu_custom_call" | custom-call | flops 536870912 | bytes 12582912 | tf_op jit(solution)/shard_map/merge/pallas_call | solution.py:219
  57.6 0.0 collective-permute-done.8
  57.7 0.1 pad_maximum_fusion.2.rest_0_
  57.7 0.0 collective-permute-done.14.rest_2_
  57.8 3.2 %final.1 = bf16[512,16,128]{2,1,0:T(8,128)(2,1)} custom-call(s32[1]{0:T(128)} %bitcast.place_ref, bf16[4,8,384,256]{3,2,1,0:T(8,128)(2,1)S(1)} %get-tuple-element.23.scaled_ref, f32[4,8,128,256]{3,2,1,0:T(8,128)S(1)} %get-tuple-element.24.a_ref, bf16[16,128,128]{2,1,0:T(8,128)(2,1)S(1)} %pad_maximum_fusion.2.rest_0_, ...), custom_call_target="tpu_custom_call" | custom-call | flops 805306368 | bytes 12582912 | tf_op jit(solution)/shard_map/final/pallas_call | solution.py:269
  (10 shorter events, 0.3 us)
Async XLA Ops:
  2.8 20.6 %copy-start = (f32[18,16,512]{2,1,0:T(8,128)S(1)}, f32[18,16,512]{2,1,0:T(8,128)}, u32[]{:S(2)}) copy-start(f32[18,16,512]{2,1,0:T(8,128)} %w_ref.5) | copy-start | bytes 1769476
  2.9 8.6 %collective-permute-start = (bf16[4,128,128]{2,1,0:T(8,128)(2,1)S(1)}, bf16[4,128,128]{2,1,0:T(8,128)(2,1)S(1)}, u32[]{:S(2)}, u32[]{:S(2)}) collective-permute-start(bf16[4,128,128]{2,1,0:T(8,128)(2,1)S(1)} %get-tuple-element.33), channel_id=1, source_target_pairs={{0,1},{1,0},{2,3},{3,2},{4,5},{5,4},{6,7},{7,6},{8,9},{9,8},{10,11... | collective-permute-start | bytes 393224 | tf_op jit(solution)/shard_map/ppermute | solution.py:290
  5.9 7.3 %collective-permute-start.3 = (bf16[4,128,128]{2,1,0:T(8,128)(2,1)S(1)}, bf16[4,128,128]{2,1,0:T(8,128)(2,1)S(1)}, u32[]{:S(2)}, u32[]{:S(2)}) collective-permute-start(bf16[4,128,128]{2,1,0:T(8,128)(2,1)S(1)} %get-tuple-element.31), channel_id=1, source_target_pairs={{0,3},{1,2},{2,1},{3,0},{4,7},{5,6},{6,5},{7,4},{8,11},{9,10},{10,... | collective-permute-start | bytes 393224 | tf_op jit(solution)/shard_map/ppermute | solution.py:290
  7.4 6.1 %collective-permute-start.2 = (bf16[4,128,128]{2,1,0:T(8,128)(2,1)S(1)}, bf16[4,128,128]{2,1,0:T(8,128)(2,1)S(1)}, u32[]{:S(2)}, u32[]{:S(2)}) collective-permute-start(bf16[4,128,128]{2,1,0:T(8,128)(2,1)S(1)} %get-tuple-element.30), channel_id=1, source_target_pairs={{0,2},{1,3},{2,0},{3,1},{4,6},{5,7},{6,4},{7,5},{8,10},{9,11},{10,... | collective-permute-start | bytes 393224 | tf_op jit(solution)/shard_map/ppermute | solution.py:290
  13.6 8.2 %collective-permute-start.6 = (bf16[4,128,128]{2,1,0:T(8,128)(2,1)S(1)}, bf16[4,128,128]{2,1,0:T(8,128)(2,1)S(1)}, u32[]{:S(2)}, u32[]{:S(2)}) collective-permute-start(bf16[4,128,128]{2,1,0:T(8,128)(2,1)S(1)} %get-tuple-element.25), channel_id=1, source_target_pairs={{0,4},{1,5},{2,6},{3,7},{4,0},{5,1},{6,2},{7,3},{8,12},{9,13},{10,... | collective-permute-start | bytes 393224 | tf_op jit(solution)/shard_map/ppermute | solution.py:290
  21.9 12.2 %collective-permute-start.9 = (bf16[4,128,128]{2,1,0:T(8,128)(2,1)S(1)}, bf16[4,128,128]{2,1,0:T(8,128)(2,1)S(1)}, u32[]{:S(2)}, u32[]{:S(2)}) collective-permute-start(bf16[4,128,128]{2,1,0:T(8,128)(2,1)S(1)} %fusion.1), channel_id=1, source_target_pairs={{0,8},{1,9},{2,10},{3,11},{4,12},{5,13},{6,14},{7,15},{8,0},{9,1},... | collective-permute-start | bytes 393224 | tf_op jit(solution)/shard_map/ppermute | solution.py:290
  22.0 20.9 %collective-permute-start.1 = (bf16[12,128,128]{2,1,0:T(8,128)(2,1)S(1)}, bf16[12,128,128]{2,1,0:T(8,128)(2,1)S(1)}, u32[]{:S(2)}, u32[]{:S(2)}) collective-permute-start(bf16[12,128,128]{2,1,0:T(8,128)(2,1)S(1)} %pad_maximum_fusion.4), channel_id=1, source_target_pairs={{0,1},{1,0},{2,3},{3,2},{4,5},{5,4},{6,7},{7,6},{8,9},{9,8},{10,11... | collective-permute-start | bytes 1179656 | tf_op jit(solution)/shard_map/ppermute | solution.py:290
  32.8 5.6 %collective-permute-start.4 = (bf16[4,128,128]{2,1,0:T(8,128)(2,1)S(1)}, bf16[4,128,128]{2,1,0:T(8,128)(2,1)S(1)}, u32[]{:S(2)}, u32[]{:S(2)}) collective-permute-start(bf16[4,128,128]{2,1,0:T(8,128)(2,1)S(1)} %get-tuple-element.22), channel_id=1, source_target_pairs={{0,1},{1,0},{2,3},{3,2},{4,5},{5,4},{6,7},{7,6},{8,9},{9,8},{10,11... | collective-permute-start | bytes 393224 | tf_op jit(solution)/shard_map/ppermute | solution.py:290
  33.5 5.7 %collective-permute-start.7 = (bf16[4,128,128]{2,1,0:T(8,128)(2,1)S(1)}, bf16[4,128,128]{2,1,0:T(8,128)(2,1)S(1)}, u32[]{:S(2)}, u32[]{:S(2)}) collective-permute-start(bf16[4,128,128]{2,1,0:T(8,128)(2,1)S(1)} %collective-permute-done.6), channel_id=1, source_target_pairs={{0,2},{1,3},{2,0},{3,1},{4,6},{5,7},{6,4},{7,5},{8,10},{9,11},{10,... | collective-permute-start | bytes 393224 | tf_op jit(solution)/shard_map/ppermute | solution.py:290
  34.1 6.2 %collective-permute-start.10 = (bf16[4,128,128]{2,1,0:T(8,128)(2,1)S(1)}, bf16[4,128,128]{2,1,0:T(8,128)(2,1)S(1)}, u32[]{:S(2)}, u32[]{:S(2)}) collective-permute-start(bf16[4,128,128]{2,1,0:T(8,128)(2,1)S(1)} %add_convert_fusion), channel_id=1, source_target_pairs={{0,16},{1,17},{2,18},{3,19},{4,20},{5,21},{6,22},{7,23},{8,24},{9,... | collective-permute-start | bytes 393224 | tf_op jit(solution)/shard_map/ppermute | solution.py:290
  38.5 13.9 %collective-permute-start.5 = (bf16[8,128,128]{2,1,0:T(8,128)(2,1)S(1)}, bf16[8,128,128]{2,1,0:T(8,128)(2,1)S(1)}, u32[]{:S(2)}, u32[]{:S(2)}) collective-permute-start(bf16[8,128,128]{2,1,0:T(8,128)(2,1)S(1)} %pad_maximum_fusion.5), channel_id=1, source_target_pairs={{0,2},{1,3},{2,0},{3,1},{4,6},{5,7},{6,4},{7,5},{8,10},{9,11},{10,... | collective-permute-start | bytes 786440 | tf_op jit(solution)/shard_map/ppermute | solution.py:290
  39.2 18.4 %collective-permute-start.8 = (bf16[8,128,128]{2,1,0:T(8,128)(2,1)S(1)}, bf16[8,128,128]{2,1,0:T(8,128)(2,1)S(1)}, u32[]{:S(2)}, u32[]{:S(2)}) collective-permute-start(bf16[8,128,128]{2,1,0:T(8,128)(2,1)S(1)} %pad_maximum_fusion.6), channel_id=1, source_target_pairs={{0,1},{1,0},{2,3},{3,2},{4,5},{5,4},{6,7},{7,6},{8,9},{9,8},{10,11... | collective-permute-start | bytes 786440 | tf_op jit(solution)/shard_map/ppermute | solution.py:290
  40.3 10.2 %collective-permute-start.13 = (bf16[4,128,128]{2,1,0:T(8,128)(2,1)S(1)}, bf16[4,128,128]{2,1,0:T(8,128)(2,1)S(1)}, u32[]{:S(2)}, u32[]{:S(2)}) collective-permute-start(bf16[4,128,128]{2,1,0:T(8,128)(2,1)S(1)} %broadcast_select_fusion), channel_id=1, source_target_pairs={{0,3},{1,2},{2,1},{3,0},{4,7},{5,6},{6,5},{7,4},{8,11},{9,10},{10,... | collective-permute-start | bytes 393224 | tf_op jit(solution)/shard_map/ppermute | solution.py:290
  42.2 9.5 %collective-permute-start.12 = (bf16[4,128,128]{2,1,0:T(8,128)(2,1)S(1)}, bf16[4,128,128]{2,1,0:T(8,128)(2,1)S(1)}, u32[]{:S(2)}, u32[]{:S(2)}) collective-permute-start(bf16[4,128,128]{2,1,0:T(8,128)(2,1)S(1)} %broadcast_select_fusion), channel_id=1, source_target_pairs={{0,2},{1,3},{2,0},{3,1},{4,6},{5,7},{6,4},{7,5},{8,10},{9,11},{10,... | collective-permute-start | bytes 393224 | tf_op jit(solution)/shard_map/ppermute | solution.py:290
  42.9 9.3 %collective-permute-start.11 = (bf16[4,128,128]{2,1,0:T(8,128)(2,1)S(1)}, bf16[4,128,128]{2,1,0:T(8,128)(2,1)S(1)}, u32[]{:S(2)}, u32[]{:S(2)}) collective-permute-start(bf16[4,128,128]{2,1,0:T(8,128)(2,1)S(1)} %broadcast_select_fusion), channel_id=1, source_target_pairs={{0,1},{1,0},{2,3},{3,2},{4,5},{5,4},{6,7},{7,6},{8,9},{9,8},{10,11... | collective-permute-start | bytes 393224 | tf_op jit(solution)/shard_map/ppermute | solution.py:290
  52.3 5.5 %collective-permute-start.14 = (bf16[16,128,128]{2,1,0:T(8,128)(2,1)S(1)}, bf16[16,128,128]{2,1,0:T(8,128)(2,1)S(1)}, u32[]{:S(2)}, u32[]{:S(2)}) collective-permute-start(bf16[16,128,128]{2,1,0:T(8,128)(2,1)S(1)} %pad_maximum_fusion.3.rest_1_), channel_id=1, source_target_pairs={{0,8},{1,9},{2,10},{3,11},{4,12},{5,13},{6,14},{7,15},{8,0},{9,1},... | collective-permute-start | bytes 1572872 | tf_op jit(solution)/shard_map/ppermute | solution.py:290

commit v2 on v1

--- a/solution.py
+++ b/solution.py
@@ -189,7 +189,7 @@
     above, low, top = late
     bit = lambda g: (place >> g & 1).astype(F32)
     level = lambda g, c: (above + g, c * 2.0 ** (-0.5 * (above + g)))
-    tail = [gain_row(place, above + g, g) for g in range(2, top) if g != low]
+    tail = [gain_row(place, above + g, g) for g in range(1, top) if g != low]
     tail.append([level(low, bit(low)), level(top, bit(top) * (1.0 - bit(low)))])
     tail.append([level(top, bit(top) * bit(low))])
     unit = pl.program_id(0)
@@ -246,42 +246,46 @@
     )(place, *turned, *accs, level_weights, *buckets)
 
 
-def final_kernel(blocks, place_ref, scaled_ref, a_ref, *rest):
+def final_kernel(blocks, part, place_ref, scaled_ref, a_ref, *rest):
     refs, out_ref = rest[:-1], rest[-1]
-    unit = pl.program_id(0)
+    place = place_ref[0]
+    unit = pl.program_id(0) * blocks + ((place >> 1 & 1) ^ part)
     block = scaled_ref.shape[1]
-    quarter = refs[0].shape[0] // 4
+    quarter = block // 2
+    if part:
+        refs = refs[:-1]
     done = []
     for h in range(block):
-        spot = unit % blocks * block + h
-        spot = (spot // quarter ^ (place_ref[0] & 3)) * quarter + spot % quarter
+        spot = (h // quarter ^ (place & 1)) * quarter + h % quarter
         wide = jnp.concatenate([ref[spot] for ref in refs], axis=1)
         total = a_ref[unit, h] + jnp.dot(wide, scaled_ref[unit, h], preferred_element_type=F32)
         done.append(total.T.astype(BF16))
     out_ref[...] = jnp.swapaxes(jnp.stack(done), 0, 1)
 
 
-def final_part(place, scaled, acc, buckets):
+def final_part(part, place, scaled, acc, buckets, before):
     units, block, dim, tile = acc.shape
     blocks = units // 2
-    heads = block * blocks
     whole = pl.BlockSpec(memory_space=pltpu.VMEM)
+    kept = [] if before is None else [before]
     return pl.pallas_call(
-        functools.partial(final_kernel, blocks),
+        functools.partial(final_kernel, blocks, part),
         grid_spec=scalar_grid(
-            (units,),
-            [whole, whole] + [whole] * len(buckets),
-            pl.BlockSpec((tile, block, dim), lambda i, p: (i // blocks, i % blocks, 0)),
-        ),
-        out_shape=jax.ShapeDtypeStruct((2 * tile, heads, dim), BF16),
-        name="final",
+            (2,),
+            [whole, whole]
+            + [whole] * len(buckets)
+            + [pl.BlockSpec(memory_space=pl.ANY)] * len(kept),
+            pl.BlockSpec((tile, block, dim), lambda i, p: (i, (p[0] >> 1 & 1) ^ part, 0)),
+        ),
+        out_shape=jax.ShapeDtypeStruct((2 * tile, blocks * block, dim), BF16),
+        input_output_aliases={3 + len(buckets): 0} if kept else {},
         compiler_params=pltpu.CompilerParams(vmem_limit_bytes=FINAL_VMEM),
         cost_estimate=pl.CostEstimate(
-            flops=2 * len(buckets) * units * block * tile * dim * dim,
-            bytes_accessed=12 * units * block * tile * dim,
+            flops=len(buckets) * units * block * tile * dim * dim,
+            bytes_accessed=6 * units * block * tile * dim,
             transcendentals=0,
         ),
-    )(place, scaled, acc, *buckets)
+    )(place, scaled, acc, *buckets, *kept)
 
 
 def exchange(value, mask):
@@ -310,21 +314,18 @@
 
     def gather_late(g):
         a = pieces[g]
-        if g % 2:
-            pair = jnp.concatenate([a, exchange(a, 1)])
-            return jnp.concatenate([pair, exchange(pair, 2)])
-        b = exchange(a, 2)
-        twin = exchange(jnp.concatenate([a, b]), 1)
-        return jnp.concatenate([a, twin[:quarter], b, twin[quarter:]])
+        twin = exchange(a, 1)
+        pair = jnp.concatenate([a, twin])
+        return pair, exchange(pair, 2)
 
     low, top = inner_depth, depth - 1
-    buckets = [zero] + [gather_late(g) for g in range(1, top) if g != low]
+    buckets = [gather_late(g) for g in range(1, top) if g != low]
     chosen = jnp.where((place >> low & 1) == 1, pieces[low], pieces[top])
-    got = {m: exchange(chosen, m) for m in (3, 2, 1)}
-    full = jnp.concatenate([chosen, got[1], got[2], got[3]])
+    got = {m: exchange(chosen, m) for m in (1, 3, 2)}
+    full = jnp.concatenate([chosen, got[1]]), jnp.concatenate([got[2], got[3]])
     buckets.append(full)
-    buckets.append(exchange(full, 1 << low))
-    return buckets
+    buckets.append([exchange(side, 1 << low) for side in full])
+    return zero, buckets
 
 
 def per_device(queries, key_vectors, value_vectors, level_weights):
@@ -337,7 +338,7 @@
     far = lambda x: pltpu.with_memory_space_constraint(x, pltpu.HBM)
     queries, key_vectors, value_vectors = map(far, (queries, key_vectors, value_vectors))
     state, first = block_states(where, key_vectors, value_vectors)
-    buckets = exchange_states(state, place, inner_depth, depth)
+    zero, buckets = exchange_states(state, place, inner_depth, depth)
     above = local_depth + 1
     units = 2 * queries.shape[1] // HEAD_BLOCK
     given = (where, queries, key_vectors, value_vectors, level_weights, first)
@@ -349,12 +350,15 @@
         (far(flat0), far(flat1)),
         (far(acc0), far(acc1)),
         level_weights,
-        buckets[:2],
-        ((above, 0), (above + 1, 1)),
+        [zero],
+        ((above, 0),),
         (above, inner_depth, depth - 1),
-        len(buckets) - 2,
+        len(buckets),
     )
-    return final_part(where, scaled, acc, buckets[2:])
+    out = None
+    for part in range(2):
+        out = final_part(part, where, scaled, acc, [b[part] for b in buckets], out)
+    return out
 
 
 def solution(mesh):

time: 61.2 us -> 64.9 us (1.060)
  waiting for transfers between devices: 22.5 us -> 25.3 us
    ppermute x15 -> x16, waiting for transfers between devices: 22.5 us -> 25.3 us  [exchange(): return lax.ppermute(value, AXES, pairs)]
    pallas_call x1 -> x2, Pallas kernels: 3.21 us -> 3.94 us  [final_part(): pl.pallas_call(functools.partial(final_kernel, blocks, part), grid_spec=s...]
    ppermute x15 -> x16, starting transfers between devices: 17.1 us -> 17.6 us  [exchange(): return lax.ppermute(value, AXES, pairs)]
  transfers between devices with their start and end apart: 15 -> 16, of which waited for: 8 -> 9; matrix products, arithmetic and copies ran while one was open for 1% -> 0% of each run, Pallas kernels for 24% -> 25%
where the time goes in v2:
time: 64.9 us; the launch traced here: 64.7 us
  waiting for transfers between devices  25.3 us (39%)
  Pallas kernels  21.1 us (33%)
  starting transfers between devices  17.6 us (27%)
    ppermute x16, waiting for transfers between devices, exchange(): return lax.ppermute(value, AXES, pairs)  25.3 us
    ppermute x16, starting transfers between devices, exchange(): return lax.ppermute(value, AXES, pairs)  17.6 us
    pallas_call x2, Pallas kernels, local_part(): pl.pallas_call(functools.partial(local_kernel, start, blocks), grid_spec=...  9.42 us
    pallas_call x1, Pallas kernels, merge_part(): pl.pallas_call(functools.partial(merge_kernel, levels, late, blocks, spli...  4.96 us
    pallas_call x2, Pallas kernels, final_part(): pl.pallas_call(functools.partial(final_kernel, blocks, part), grid_spec=s...  3.94 us
    pallas_call x1, Pallas kernels, block_states(): pl.pallas_call(state_kernel, grid_spec=scalar_grid((2,), [source, source]...  2.79 us
  transfers between devices with their start and end apart: 16, of which 9 were waited for; matrix products, arithmetic and copies ran while one was open for 0% of the time, Pallas kernels for 25%

profile of v2, /device:TPU:0, one launch (start us, length us, event | category | flops | bytes accessed | tf_op | source)
XLA Modules:
  0.0 64.7 jit_solution(3318091975767116279)
XLA Ops:
  0.0 2.8 %states.1 = (bf16[16,128,128]{2,1,0:T(8,128)(2,1)S(1)}, bf16[16,128,128]{2,1,0:T(8,128)(2,1)S(1)}) custom-call(s32[1]{0:T(128)} %bitcast.place_ref, bf16[512,16,128]{2,1,0:T(8,128)(2,1)} %k_ref.5, bf16[512,16,128]{2,1,0:T(8,128)(2,1)} %v_ref.5), custom_call_target="tpu_custom_call" | custom-call | flops 268435456 | bytes 4194304 | tf_op jit(solution)/shard_map/states/pallas_call | solution.py:50
  2.8 0.0 copy-start
  2.9 3.0 %collective-permute-start = (bf16[4,128,128]{2,1,0:T(8,128)(2,1)S(1)}, bf16[4,128,128]{2,1,0:T(8,128)(2,1)S(1)}, u32[]{:S(2)}, u32[]{:S(2)}) collective-permute-start(bf16[4,128,128]{2,1,0:T(8,128)(2,1)S(1)} %get-tuple-element.33), channel_id=1, source_target_pairs={{0,1},{1,0},{2,3},{3,2},{4,5},{5,4},{6,7},{7,6},{8,9},{9,8},{10,11... | collective-permute-start | bytes 393224 | tf_op jit(solution)/shard_map/ppermute | solution.py:294
  5.9 1.5 %collective-permute-start.3 = (bf16[4,128,128]{2,1,0:T(8,128)(2,1)S(1)}, bf16[4,128,128]{2,1,0:T(8,128)(2,1)S(1)}, u32[]{:S(2)}, u32[]{:S(2)}) collective-permute-start(bf16[4,128,128]{2,1,0:T(8,128)(2,1)S(1)} %get-tuple-element.31), channel_id=1, source_target_pairs={{0,3},{1,2},{2,1},{3,0},{4,7},{5,6},{6,5},{7,4},{8,11},{9,10},{10,... | collective-permute-start | bytes 393224 | tf_op jit(solution)/shard_map/ppermute | solution.py:294
  7.4 0.0 collective-permute-start.2
  7.5 4.0 %collective-permute-done = bf16[4,128,128]{2,1,0:T(8,128)(2,1)S(1)} collective-permute-done((bf16[4,128,128]{2,1,0:T(8,128)(2,1)S(1)}, bf16[4,128,128]{2,1,0:T(8,128)(2,1)S(1)}, u32[]{:S(2)}, u32[]{:S(2)}) %collective-permute-start) | collective-permute-done | bytes 131104 | tf_op jit(solution)/shard_map/ppermute | solution.py:294
  11.5 1.7 %collective-permute-done.3 = bf16[4,128,128]{2,1,0:T(8,128)(2,1)S(1)} collective-permute-done((bf16[4,128,128]{2,1,0:T(8,128)(2,1)S(1)}, bf16[4,128,128]{2,1,0:T(8,128)(2,1)S(1)}, u32[]{:S(2)}, u32[]{:S(2)}) %collective-permute-start.3) | collective-permute-done | bytes 131104 | tf_op jit(solution)/shard_map/ppermute | solution.py:294
  13.2 0.4 collective-permute-done.2
  13.5 0.1 fusion.2
  13.6 2.8 %collective-permute-start.6 = (bf16[4,128,128]{2,1,0:T(8,128)(2,1)S(1)}, bf16[4,128,128]{2,1,0:T(8,128)(2,1)S(1)}, u32[]{:S(2)}, u32[]{:S(2)}) collective-permute-start(bf16[4,128,128]{2,1,0:T(8,128)(2,1)S(1)} %get-tuple-element.25), channel_id=1, source_target_pairs={{0,4},{1,5},{2,6},{3,7},{4,0},{5,1},{6,2},{7,3},{8,12},{9,13},{10,... | collective-permute-start | bytes 393224 | tf_op jit(solution)/shard_map/ppermute | solution.py:294
  16.5 5.4 %collective-permute-done.6 = bf16[4,128,128]{2,1,0:T(8,128)(2,1)S(1)} collective-permute-done((bf16[4,128,128]{2,1,0:T(8,128)(2,1)S(1)}, bf16[4,128,128]{2,1,0:T(8,128)(2,1)S(1)}, u32[]{:S(2)}, u32[]{:S(2)}) %collective-permute-start.6) | collective-permute-done | bytes 131104 | tf_op jit(solution)/shard_map/ppermute | solution.py:294
  21.9 0.1 collective-permute-start.9
  22.0 1.4 %collective-permute-start.1 = (bf16[12,128,128]{2,1,0:T(8,128)(2,1)S(1)}, bf16[12,128,128]{2,1,0:T(8,128)(2,1)S(1)}, u32[]{:S(2)}, u32[]{:S(2)}) collective-permute-start(bf16[12,128,128]{2,1,0:T(8,128)(2,1)S(1)} %pad_maximum_fusion.1), channel_id=1, source_target_pairs={{0,1},{1,0},{2,3},{3,2},{4,5},{5,4},{6,7},{7,6},{8,9},{9,8},{10,11... | collective-permute-start | bytes 1179656 | tf_op jit(solution)/shard_map/ppermute | solution.py:294
  23.4 0.0 copy-done
  23.4 3.3 %shard_map.47 = (f32[1,8,128,256]{3,2,1,0:T(8,128)}, bf16[1,8,256,128]{3,2,1,0:T(8,128)(2,1)}) custom-call(s32[1]{0:T(128)} %bitcast.place_ref, bf16[512,16,128]{2,1,0:T(8,128)(2,1)} %q_ref.3, bf16[512,16,128]{2,1,0:T(8,128)(2,1)} %k_ref.5, bf16[512,16,128]{2,1,0:T(8,128)(2,1)} %v_ref.5, f32[18,16,512]{2,1,0:T(8,128)S(1)} %copy-done, ...), custom_call_target="tpu_custom_call" | custom-call | flops 268435456 | bytes 3145728 | tf_op jit(solution)/shard_map/pallas_call | solution.py:134
  26.7 6.1 %shard_map.46 = (f32[3,8,128,256]{3,2,1,0:T(8,128)}, bf16[3,8,256,128]{3,2,1,0:T(8,128)(2,1)}) custom-call(s32[1]{0:T(128)} %bitcast.place_ref, bf16[512,16,128]{2,1,0:T(8,128)(2,1)} %q_ref.3, bf16[512,16,128]{2,1,0:T(8,128)(2,1)} %k_ref.5, bf16[512,16,128]{2,1,0:T(8,128)(2,1)} %v_ref.5, f32[18,16,512]{2,1,0:T(8,128)S(1)} %copy-done, ...), custom_call_target="tpu_custom_call" | custom-call | flops 805306368 | bytes 9437184 | tf_op jit(solution)/shard_map/pallas_call | solution.py:134
  32.8 0.7 %collective-permute-start.4 = (bf16[4,128,128]{2,1,0:T(8,128)(2,1)S(1)}, bf16[4,128,128]{2,1,0:T(8,128)(2,1)S(1)}, u32[]{:S(2)}, u32[]{:S(2)}) collective-permute-start(bf16[4,128,128]{2,1,0:T(8,128)(2,1)S(1)} %get-tuple-element.24), channel_id=1, source_target_pairs={{0,1},{1,0},{2,3},{3,2},{4,5},{5,4},{6,7},{7,6},{8,9},{9,8},{10,11... | collective-permute-start | bytes 393224 | tf_op jit(solution)/shard_map/ppermute | solution.py:294
  33.5 0.0 collective-permute-done.9
  33.6 1.5 %collective-permute-start.10 = (bf16[4,128,128]{2,1,0:T(8,128)(2,1)S(1)}, bf16[4,128,128]{2,1,0:T(8,128)(2,1)S(1)}, u32[]{:S(2)}, u32[]{:S(2)}) collective-permute-start(bf16[4,128,128]{2,1,0:T(8,128)(2,1)S(1)} %add_convert_fusion), channel_id=1, source_target_pairs={{0,16},{1,17},{2,18},{3,19},{4,20},{5,21},{6,22},{7,23},{8,24},{9,... | collective-permute-start | bytes 393224 | tf_op jit(solution)/shard_map/ppermute | solution.py:294
  35.0 3.4 %collective-permute-done.4 = bf16[4,128,128]{2,1,0:T(8,128)(2,1)S(1)} collective-permute-done((bf16[4,128,128]{2,1,0:T(8,128)(2,1)S(1)}, bf16[4,128,128]{2,1,0:T(8,128)(2,1)S(1)}, u32[]{:S(2)}, u32[]{:S(2)}) %collective-permute-start.4) | collective-permute-done | bytes 131104 | tf_op jit(solution)/shard_map/ppermute | solution.py:294
  38.5 0.7 %collective-permute-start.5 = (bf16[8,128,128]{2,1,0:T(8,128)(2,1)S(1)}, bf16[8,128,128]{2,1,0:T(8,128)(2,1)S(1)}, u32[]{:S(2)}, u32[]{:S(2)}) collective-permute-start(bf16[8,128,128]{2,1,0:T(8,128)(2,1)S(1)} %constant_dynamic-update-slice_fusion.rest_0_), channel_id=1, source_target_pairs={{0,2},{1,3},{2,0},{3,1},{4,6},{5,7},{6,4},{7,5},{8,10},{9,11},{10,... | collective-permute-start | bytes 786440 | tf_op jit(solution)/shard_map/ppermute | solution.py:294
  39.2 0.5 collective-permute-start.7
  39.7 0.0 collective-permute-done.10
  39.8 1.5 %collective-permute-start.11 = (bf16[4,128,128]{2,1,0:T(8,128)(2,1)S(1)}, bf16[4,128,128]{2,1,0:T(8,128)(2,1)S(1)}, u32[]{:S(2)}, u32[]{:S(2)}) collective-permute-start(bf16[4,128,128]{2,1,0:T(8,128)(2,1)S(1)} %broadcast_select_fusion), channel_id=1, source_target_pairs={{0,2},{1,3},{2,0},{3,1},{4,6},{5,7},{6,4},{7,5},{8,10},{9,11},{10,... | collective-permute-start | bytes 393224 | tf_op jit(solution)/shard_map/ppermute | solution.py:294
  41.3 1.5 %collective-permute-start.12 = (bf16[4,128,128]{2,1,0:T(8,128)(2,1)S(1)}, bf16[4,128,128]{2,1,0:T(8,128)(2,1)S(1)}, u32[]{:S(2)}, u32[]{:S(2)}) collective-permute-start(bf16[4,128,128]{2,1,0:T(8,128)(2,1)S(1)} %broadcast_select_fusion), channel_id=1, source_target_pairs={{0,3},{1,2},{2,1},{3,0},{4,7},{5,6},{6,5},{7,4},{8,11},{9,10},{10,... | collective-permute-start | bytes 393224 | tf_op jit(solution)/shard_map/ppermute | solution.py:294
  42.9 1.3 %collective-permute-done.7 = bf16[4,128,128]{2,1,0:T(8,128)(2,1)S(1)} collective-permute-done((bf16[4,128,128]{2,1,0:T(8,128)(2,1)S(1)}, bf16[4,128,128]{2,1,0:T(8,128)(2,1)S(1)}, u32[]{:S(2)}, u32[]{:S(2)}) %collective-permute-start.7) | collective-permute-done | bytes 131104 | tf_op jit(solution)/shard_map/ppermute | solution.py:294
  44.2 1.4 %collective-permute-start.8 = (bf16[8,128,128]{2,1,0:T(8,128)(2,1)S(1)}, bf16[8,128,128]{2,1,0:T(8,128)(2,1)S(1)}, u32[]{:S(2)}, u32[]{:S(2)}) collective-permute-start(bf16[8,128,128]{2,1,0:T(8,128)(2,1)S(1)} %constant_dynamic-update-slice_fusion.2.rest_1_), channel_id=1, source_target_pairs={{0,2},{1,3},{2,0},{3,1},{4,6},{5,7},{6,4},{7,5},{8,10},{9,11},{10,... | collective-permute-start | bytes 786440 | tf_op jit(solution)/shard_map/ppermute | solution.py:294
  45.6 4.9 %collective-permute-done.11 = bf16[4,128,128]{2,1,0:T(8,128)(2,1)S(1)} collective-permute-done((bf16[4,128,128]{2,1,0:T(8,128)(2,1)S(1)}, bf16[4,128,128]{2,1,0:T(8,128)(2,1)S(1)}, u32[]{:S(2)}, u32[]{:S(2)}) %collective-permute-start.11) | collective-permute-done | bytes 131104 | tf_op jit(solution)/shard_map/ppermute | solution.py:294
  50.5 0.7 %collective-permute-start.14 = (bf16[4,128,128]{2,1,0:T(8,128)(2,1)S(1)}, bf16[4,128,128]{2,1,0:T(8,128)(2,1)S(1)}, u32[]{:S(2)}, u32[]{:S(2)}) collective-permute-start(bf16[4,128,128]{2,1,0:T(8,128)(2,1)S(1)} %broadcast_select_fusion), channel_id=1, source_target_pairs={{0,1},{1,0},{2,3},{3,2},{4,5},{5,4},{6,7},{7,6},{8,9},{9,8},{10,11... | collective-permute-start | bytes 393224 | tf_op jit(solution)/shard_map/ppermute | solution.py:294
  51.2 2.2 %collective-permute-done.12 = bf16[4,128,128]{2,1,0:T(8,128)(2,1)S(1)} collective-permute-done((bf16[4,128,128]{2,1,0:T(8,128)(2,1)S(1)}, bf16[4,128,128]{2,1,0:T(8,128)(2,1)S(1)}, u32[]{:S(2)}, u32[]{:S(2)}) %collective-permute-start.12) | collective-permute-done | bytes 131104 | tf_op jit(solution)/shard_map/ppermute | solution.py:294
  53.5 0.1 collective-permute-start.13
  53.5 2.0 %collective-permute-done.14 = bf16[4,128,128]{2,1,0:T(8,128)(2,1)S(1)} collective-permute-done((bf16[4,128,128]{2,1,0:T(8,128)(2,1)S(1)}, bf16[4,128,128]{2,1,0:T(8,128)(2,1)S(1)}, u32[]{:S(2)}, u32[]{:S(2)}) %collective-permute-start.14) | collective-permute-done | bytes 131104 | tf_op jit(solution)/shard_map/ppermute | solution.py:294
  55.5 0.1 collective-permute-start.15
  55.6 0.0 collective-permute-done.1
  55.7 0.1 pad_maximum_fusion.rest_0_
  55.7 5.0 %merge.1 = (f32[4,8,128,256]{3,2,1,0:T(8,128)S(1)}, bf16[4,8,512,256]{3,2,1,0:T(8,128)(2,1)S(1)}) custom-call(s32[1]{0:T(128)} %bitcast.place_ref, bf16[3,8,256,128]{3,2,1,0:T(8,128)(2,1)} %get-tuple-element.17.qa_ref, bf16[1,8,256,128]{3,2,1,0:T(8,128)(2,1)} %get-tuple-element.18.qb_ref, f32[3,8,128,256]{3,2,1,0:T(8,128)} %get-tuple-element.19.aa_ref, ...), custom_call_target="tpu_custom_call" | custom-call | flops 268435456 | bytes 12582912 | tf_op jit(solution)/shard_map/merge/pallas_call | solution.py:219
  60.7 0.0 collective-permute-done.15.rest_3_
  60.7 2.0 %shard_map.48.rest_4_ = bf16[512,16,128]{2,1,0:T(8,128)(2,1)} custom-call(s32[1]{0:T(128)} %bitcast.place_ref, bf16[4,8,512,256]{3,2,1,0:T(8,128)(2,1)S(1)} %get-tuple-element.22.scaled_ref, f32[4,8,128,256]{3,2,1,0:T(8,128)S(1)} %get-tuple-element.23.a_ref, bf16[8,128,128]{2,1,0:T(8,128)(2,1)S(1)} %constant_dynamic-update-slice_fusion.rest_0_, ...), custom_call_target="tpu_custom_call" | custom-call | flops 536870912 | bytes 6291456 | tf_op jit(solution)/shard_map/pallas_call | solution.py:271
  62.7 0.0 collective-permute-done.5.rest_0_
  62.7 0.0 collective-permute-done.8.rest_1_
  62.7 0.0 collective-permute-done.13.rest_3_
  62.7 2.0 %shard_map.49 = bf16[512,16,128]{2,1,0:T(8,128)(2,1)} custom-call(s32[1]{0:T(128)} %bitcast.place_ref, bf16[4,8,512,256]{3,2,1,0:T(8,128)(2,1)S(1)} %get-tuple-element.22.scaled_ref, f32[4,8,128,256]{3,2,1,0:T(8,128)S(1)} %get-tuple-element.23.a_ref, bf16[8,128,128]{2,1,0:T(8,128)(2,1)S(1)} %collective-permute-done.5.rest_0_, ...), custom_call_target="tpu_custom_call", output_to_operand_aliasing={{}: (7, {})} | custom-call | flops 536870912 | bytes 6291456 | tf_op jit(solution)/shard_map/pallas_call | solution.py:271
  (14 shorter events, 0.3 us)
Async XLA Ops:
  2.8 20.6 %copy-start = (f32[18,16,512]{2,1,0:T(8,128)S(1)}, f32[18,16,512]{2,1,0:T(8,128)}, u32[]{:S(2)}) copy-start(f32[18,16,512]{2,1,0:T(8,128)} %w_ref.5) | copy-start | bytes 1769476
  2.9 8.6 %collective-permute-start = (bf16[4,128,128]{2,1,0:T(8,128)(2,1)S(1)}, bf16[4,128,128]{2,1,0:T(8,128)(2,1)S(1)}, u32[]{:S(2)}, u32[]{:S(2)}) collective-permute-start(bf16[4,128,128]{2,1,0:T(8,128)(2,1)S(1)} %get-tuple-element.33), channel_id=1, source_target_pairs={{0,1},{1,0},{2,3},{3,2},{4,5},{5,4},{6,7},{7,6},{8,9},{9,8},{10,11... | collective-permute-start | bytes 393224 | tf_op jit(solution)/shard_map/ppermute | solution.py:294
  5.9 7.3 %collective-permute-start.3 = (bf16[4,128,128]{2,1,0:T(8,128)(2,1)S(1)}, bf16[4,128,128]{2,1,0:T(8,128)(2,1)S(1)}, u32[]{:S(2)}, u32[]{:S(2)}) collective-permute-start(bf16[4,128,128]{2,1,0:T(8,128)(2,1)S(1)} %get-tuple-element.31), channel_id=1, source_target_pairs={{0,3},{1,2},{2,1},{3,0},{4,7},{5,6},{6,5},{7,4},{8,11},{9,10},{10,... | collective-permute-start | bytes 393224 | tf_op jit(solution)/shard_map/ppermute | solution.py:294
  7.4 6.1 %collective-permute-start.2 = (bf16[4,128,128]{2,1,0:T(8,128)(2,1)S(1)}, bf16[4,128,128]{2,1,0:T(8,128)(2,1)S(1)}, u32[]{:S(2)}, u32[]{:S(2)}) collective-permute-start(bf16[4,128,128]{2,1,0:T(8,128)(2,1)S(1)} %get-tuple-element.30), channel_id=1, source_target_pairs={{0,2},{1,3},{2,0},{3,1},{4,6},{5,7},{6,4},{7,5},{8,10},{9,11},{10,... | collective-permute-start | bytes 393224 | tf_op jit(solution)/shard_map/ppermute | solution.py:294
  13.6 8.2 %collective-permute-start.6 = (bf16[4,128,128]{2,1,0:T(8,128)(2,1)S(1)}, bf16[4,128,128]{2,1,0:T(8,128)(2,1)S(1)}, u32[]{:S(2)}, u32[]{:S(2)}) collective-permute-start(bf16[4,128,128]{2,1,0:T(8,128)(2,1)S(1)} %get-tuple-element.25), channel_id=1, source_target_pairs={{0,4},{1,5},{2,6},{3,7},{4,0},{5,1},{6,2},{7,3},{8,12},{9,13},{10,... | collective-permute-start | bytes 393224 | tf_op jit(solution)/shard_map/ppermute | solution.py:294
  21.9 11.6 %collective-permute-start.9 = (bf16[4,128,128]{2,1,0:T(8,128)(2,1)S(1)}, bf16[4,128,128]{2,1,0:T(8,128)(2,1)S(1)}, u32[]{:S(2)}, u32[]{:S(2)}) collective-permute-start(bf16[4,128,128]{2,1,0:T(8,128)(2,1)S(1)} %fusion.1), channel_id=1, source_target_pairs={{0,8},{1,9},{2,10},{3,11},{4,12},{5,13},{6,14},{7,15},{8,0},{9,1},... | collective-permute-start | bytes 393224 | tf_op jit(solution)/shard_map/ppermute | solution.py:294
  22.0 33.6 %collective-permute-start.1 = (bf16[12,128,128]{2,1,0:T(8,128)(2,1)S(1)}, bf16[12,128,128]{2,1,0:T(8,128)(2,1)S(1)}, u32[]{:S(2)}, u32[]{:S(2)}) collective-permute-start(bf16[12,128,128]{2,1,0:T(8,128)(2,1)S(1)} %pad_maximum_fusion.1), channel_id=1, source_target_pairs={{0,1},{1,0},{2,3},{3,2},{4,5},{5,4},{6,7},{7,6},{8,9},{9,8},{10,11... | collective-permute-start | bytes 1179656 | tf_op jit(solution)/shard_map/ppermute | solution.py:294
  32.8 5.6 %collective-permute-start.4 = (bf16[4,128,128]{2,1,0:T(8,128)(2,1)S(1)}, bf16[4,128,128]{2,1,0:T(8,128)(2,1)S(1)}, u32[]{:S(2)}, u32[]{:S(2)}) collective-permute-start(bf16[4,128,128]{2,1,0:T(8,128)(2,1)S(1)} %get-tuple-element.24), channel_id=1, source_target_pairs={{0,1},{1,0},{2,3},{3,2},{4,5},{5,4},{6,7},{7,6},{8,9},{9,8},{10,11... | collective-permute-start | bytes 393224 | tf_op jit(solution)/shard_map/ppermute | solution.py:294
  33.6 6.2 %collective-permute-start.10 = (bf16[4,128,128]{2,1,0:T(8,128)(2,1)S(1)}, bf16[4,128,128]{2,1,0:T(8,128)(2,1)S(1)}, u32[]{:S(2)}, u32[]{:S(2)}) collective-permute-start(bf16[4,128,128]{2,1,0:T(8,128)(2,1)S(1)} %add_convert_fusion), channel_id=1, source_target_pairs={{0,16},{1,17},{2,18},{3,19},{4,20},{5,21},{6,22},{7,23},{8,24},{9,... | collective-permute-start | bytes 393224 | tf_op jit(solution)/shard_map/ppermute | solution.py:294
  38.5 24.2 %collective-permute-start.5 = (bf16[8,128,128]{2,1,0:T(8,128)(2,1)S(1)}, bf16[8,128,128]{2,1,0:T(8,128)(2,1)S(1)}, u32[]{:S(2)}, u32[]{:S(2)}) collective-permute-start(bf16[8,128,128]{2,1,0:T(8,128)(2,1)S(1)} %constant_dynamic-update-slice_fusion.rest_0_), channel_id=1, source_target_pairs={{0,2},{1,3},{2,0},{3,1},{4,6},{5,7},{6,4},{7,5},{8,10},{9,11},{10,... | collective-permute-start | bytes 786440 | tf_op jit(solution)/shard_map/ppermute | solution.py:294
  39.2 5.0 %collective-permute-start.7 = (bf16[4,128,128]{2,1,0:T(8,128)(2,1)S(1)}, bf16[4,128,128]{2,1,0:T(8,128)(2,1)S(1)}, u32[]{:S(2)}, u32[]{:S(2)}) collective-permute-start(bf16[4,128,128]{2,1,0:T(8,128)(2,1)S(1)} %collective-permute-done.6), channel_id=1, source_target_pairs={{0,1},{1,0},{2,3},{3,2},{4,5},{5,4},{6,7},{7,6},{8,9},{9,8},{10,11... | collective-permute-start | bytes 393224 | tf_op jit(solution)/shard_map/ppermute | solution.py:294
  39.8 10.8 %collective-permute-start.11 = (bf16[4,128,128]{2,1,0:T(8,128)(2,1)S(1)}, bf16[4,128,128]{2,1,0:T(8,128)(2,1)S(1)}, u32[]{:S(2)}, u32[]{:S(2)}) collective-permute-start(bf16[4,128,128]{2,1,0:T(8,128)(2,1)S(1)} %broadcast_select_fusion), channel_id=1, source_target_pairs={{0,2},{1,3},{2,0},{3,1},{4,6},{5,7},{6,4},{7,5},{8,10},{9,11},{10,... | collective-permute-start | bytes 393224 | tf_op jit(solution)/shard_map/ppermute | solution.py:294
  41.3 12.1 %collective-permute-start.12 = (bf16[4,128,128]{2,1,0:T(8,128)(2,1)S(1)}, bf16[4,128,128]{2,1,0:T(8,128)(2,1)S(1)}, u32[]{:S(2)}, u32[]{:S(2)}) collective-permute-start(bf16[4,128,128]{2,1,0:T(8,128)(2,1)S(1)} %broadcast_select_fusion), channel_id=1, source_target_pairs={{0,3},{1,2},{2,1},{3,0},{4,7},{5,6},{6,5},{7,4},{8,11},{9,10},{10,... | collective-permute-start | bytes 393224 | tf_op jit(solution)/shard_map/ppermute | solution.py:294
  44.2 18.5 %collective-permute-start.8 = (bf16[8,128,128]{2,1,0:T(8,128)(2,1)S(1)}, bf16[8,128,128]{2,1,0:T(8,128)(2,1)S(1)}, u32[]{:S(2)}, u32[]{:S(2)}) collective-permute-start(bf16[8,128,128]{2,1,0:T(8,128)(2,1)S(1)} %constant_dynamic-update-slice_fusion.2.rest_1_), channel_id=1, source_target_pairs={{0,2},{1,3},{2,0},{3,1},{4,6},{5,7},{6,4},{7,5},{8,10},{9,11},{10,... | collective-permute-start | bytes 786440 | tf_op jit(solution)/shard_map/ppermute | solution.py:294
  50.5 5.0 %collective-permute-start.14 = (bf16[4,128,128]{2,1,0:T(8,128)(2,1)S(1)}, bf16[4,128,128]{2,1,0:T(8,128)(2,1)S(1)}, u32[]{:S(2)}, u32[]{:S(2)}) collective-permute-start(bf16[4,128,128]{2,1,0:T(8,128)(2,1)S(1)} %broadcast_select_fusion), channel_id=1, source_target_pairs={{0,1},{1,0},{2,3},{3,2},{4,5},{5,4},{6,7},{7,6},{8,9},{9,8},{10,11... | collective-permute-start | bytes 393224 | tf_op jit(solution)/shard_map/ppermute | solution.py:294
  53.5 9.2 %collective-permute-start.13 = (bf16[8,128,128]{2,1,0:T(8,128)(2,1)S(1)}, bf16[8,128,128]{2,1,0:T(8,128)(2,1)S(1)}, u32[]{:S(2)}, u32[]{:S(2)}) collective-permute-start(bf16[8,128,128]{2,1,0:T(8,128)(2,1)S(1)} %constant_dynamic-update-slice_fusion.4.rest_2_), channel_id=1, source_target_pairs={{0,8},{1,9},{2,10},{3,11},{4,12},{5,13},{6,14},{7,15},{8,0},{9,1},... | collective-permute-start | bytes 786440 | tf_op jit(solution)/shard_map/ppermute | solution.py:294
  55.5 5.2 %collective-permute-start.15 = (bf16[8,128,128]{2,1,0:T(8,128)(2,1)S(1)}, bf16[8,128,128]{2,1,0:T(8,128)(2,1)S(1)}, u32[]{:S(2)}, u32[]{:S(2)}) collective-permute-start(bf16[8,128,128]{2,1,0:T(8,128)(2,1)S(1)} %pad_maximum_fusion.2.rest_2_), channel_id=1, source_target_pairs={{0,8},{1,9},{2,10},{3,11},{4,12},{5,13},{6,14},{7,15},{8,0},{9,1},... | collective-permute-start | bytes 786440 | tf_op jit(solution)/shard_map/ppermute | solution.py:294

commit v3 on v2

--- a/solution.py
+++ b/solution.py
@@ -65,7 +65,8 @@
     )(place, key_vectors, value_vectors)
 
 
-def local_kernel(start, blocks, place_ref, q_ref, k_ref, v_ref, w_ref, first_ref, acc_ref, qh_ref):
+def local_kernel(start, blocks, place_ref, q_ref, k_ref, v_ref, w_ref, first_ref, *rest):
+    acc_ref, qh_ref = rest[-2:]
     unit = start + pl.program_id(0)
     second = (unit >= blocks).astype(F32)
     tile = q_ref.shape[0]
@@ -124,10 +125,11 @@
             )
 
 
-def local_part(start, count, place, queries, key_vectors, value_vectors, level_weights, first):
+def local_part(start, count, place, queries, key_vectors, value_vectors, weights, first, kept=()):
     tokens, heads, dim = queries.shape
     tile = tokens // 2
     blocks = heads // HEAD_BLOCK
+    units = 2 * blocks
     source = pl.BlockSpec(
         (tile, HEAD_BLOCK, dim), lambda i, p: ((start + i) // blocks, (start + i) % blocks, 0)
     )
@@ -140,27 +142,29 @@
                 source,
                 source,
                 pl.BlockSpec(
-                    (level_weights.shape[0], HEAD_BLOCK, tile),
+                    (weights.shape[0], HEAD_BLOCK, tile),
                     lambda i, p: (0, (start + i) % blocks, (start + i) // blocks),
                 ),
                 pl.BlockSpec((heads, dim, dim), lambda i, p: (0, 0, 0)),
+            ]
+            + [pl.BlockSpec(memory_space=pl.ANY)] * len(kept),
+            [
+                pl.BlockSpec((None, HEAD_BLOCK, dim, tile), lambda i, p: (start + i, 0, 0, 0)),
+                pl.BlockSpec((None, HEAD_BLOCK, tile, dim), lambda i, p: (start + i, 0, 0, 0)),
             ],
-            [
-                pl.BlockSpec((None, HEAD_BLOCK, dim, tile), lambda i, p: (i, 0, 0, 0)),
-                pl.BlockSpec((None, HEAD_BLOCK, tile, dim), lambda i, p: (i, 0, 0, 0)),
-            ],
         ),
         out_shape=[
-            pltpu.HBM((count, HEAD_BLOCK, dim, tile), F32),
-            pltpu.HBM((count, HEAD_BLOCK, tile, dim), BF16),
+            pltpu.HBM((units, HEAD_BLOCK, dim, tile), F32),
+            pltpu.HBM((units, HEAD_BLOCK, tile, dim), BF16),
         ],
+        input_output_aliases={6: 0, 7: 1} if kept else {},
         compiler_params=pltpu.CompilerParams(vmem_limit_bytes=LOCAL_VMEM),
         cost_estimate=pl.CostEstimate(
             flops=4 * count * tile * tile * HEAD_BLOCK * dim,
             bytes_accessed=12 * count * tile * HEAD_BLOCK * dim,
             transcendentals=0,
         ),
-    )(place, queries, key_vectors, value_vectors, level_weights, first)
+    )(place, queries, key_vectors, value_vectors, weights, first, *kept)
 
 
 def gain_row(place, level, bit):
@@ -182,7 +186,7 @@
     return total
 
 
-def merge_kernel(levels, late, blocks, split, place_ref, qa_ref, qb_ref, aa_ref, ab_ref, w_ref, *rest):
+def merge_kernel(levels, late, blocks, place_ref, q_ref, a_ref, w_ref, *rest):
     refs, (acc_ref, scaled_ref) = rest[:-2], rest[-2:]
     place = place_ref[0]
     rows = [gain_row(place, *level) for level in levels]
@@ -194,37 +198,29 @@
     tail.append([level(top, bit(top) * bit(low))])
     unit = pl.program_id(0)
 
-    def take(q_ref, a_ref):
-        dim = q_ref.shape[2]
-        for h in range(q_ref.shape[0]):
-            acc_ref[unit, h] = a_ref[h] + bucket_sum(
-                place, unit % blocks, w_ref, q_ref, h, refs, rows
-            )
-            turned = q_ref[h].T.astype(F32)
-            for n, row in enumerate(tail):
-                gain = sum(w_ref[l, h : h + 1, :] * c for l, c in row)
-                scaled_ref[unit, h, n * dim : (n + 1) * dim, :] = (turned * gain).astype(BF16)
-
-    pl.when(unit < split)(lambda: take(qa_ref, aa_ref))
-    pl.when(unit >= split)(lambda: take(qb_ref, ab_ref))
-
-
-def merge_part(place, turned, accs, level_weights, buckets, levels, late, count):
-    split, block, tile, dim = turned[0].shape
-    units = split + turned[1].shape[0]
+    dim = q_ref.shape[2]
+    for h in range(q_ref.shape[0]):
+        acc_ref[unit, h] = a_ref[h] + bucket_sum(
+            place, unit % blocks, w_ref, q_ref, h, refs, rows
+        )
+        turned = q_ref[h].T.astype(F32)
+        for n, row in enumerate(tail):
+            gain = sum(w_ref[l, h : h + 1, :] * c for l, c in row)
+            scaled_ref[unit, h, n * dim : (n + 1) * dim, :] = (turned * gain).astype(BF16)
+
+
+def merge_part(place, turned, acc, level_weights, buckets, levels, late, count):
+    units, block, tile, dim = turned.shape
     blocks = units // 2
-    ahead = lambda i, p: (jnp.minimum(i, split - 1), 0, 0, 0)
-    after = lambda i, p: (jnp.maximum(i - split, 0), 0, 0, 0)
+    each = lambda i, p: (i, 0, 0, 0)
     whole = pl.BlockSpec(memory_space=pltpu.VMEM)
     return pl.pallas_call(
-        functools.partial(merge_kernel, levels, late, blocks, split),
+        functools.partial(merge_kernel, levels, late, blocks),
         grid_spec=scalar_grid(
             (units,),
             [
-                pl.BlockSpec((None, block, tile, dim), ahead),
-                pl.BlockSpec((None, block, tile, dim), after),
-                pl.BlockSpec((None, block, dim, tile), ahead),
-                pl.BlockSpec((None, block, dim, tile), after),
+                pl.BlockSpec((None, block, tile, dim), each),
+                pl.BlockSpec((None, block, dim, tile), each),
                 pl.BlockSpec(
                     (level_weights.shape[0], block, tile), lambda i, p: (0, i % blocks, i // blocks)
                 ),
@@ -243,7 +239,7 @@
             bytes_accessed=12 * units * block * tile * dim,
             transcendentals=0,
         ),
-    )(place, *turned, *accs, level_weights, *buckets)
+    )(place, turned, acc, level_weights, *buckets)
 
 
 def final_kernel(blocks, part, place_ref, scaled_ref, a_ref, *rest):
@@ -343,12 +339,12 @@
     units = 2 * queries.shape[1] // HEAD_BLOCK
     given = (where, queries, key_vectors, value_vectors, level_weights, first)
     split = SPLIT * units // 4
-    acc0, flat0 = local_part(0, split, *given)
-    acc1, flat1 = local_part(split, units - split, *given)
+    sums = local_part(0, split, *given)
+    acc, flat = local_part(split, units - split, *given, sums)
     acc, scaled = merge_part(
         where,
-        (far(flat0), far(flat1)),
-        (far(acc0), far(acc1)),
+        far(flat),
+        far(acc),
         level_weights,
         [zero],
         ((above, 0),),

time: 64.9 us -> 64.5 us (level)
  transfers between devices with their start and end apart: 16 -> 16, of which waited for: 9 -> 9; matrix products, arithmetic and copies ran while one was open for 0% -> 1% of each run, Pallas kernels for 25% -> 25%
where the time goes in v3:
time: 64.5 us; the launch traced here: 64.2 us
  waiting for transfers between devices  25.3 us (39%)
  Pallas kernels  20.7 us (32%)
  starting transfers between devices  17.6 us (27%)
    ppermute x16, waiting for transfers between devices, exchange(): return lax.ppermute(value, AXES, pairs)  25.3 us
    ppermute x16, starting transfers between devices, exchange(): return lax.ppermute(value, AXES, pairs)  17.6 us
    pallas_call x2, Pallas kernels, local_part(): pl.pallas_call(functools.partial(local_kernel, start, blocks), grid_spec=...  9.42 us
    pallas_call x1, Pallas kernels, merge_part(): pl.pallas_call(functools.partial(merge_kernel, levels, late, blocks), gri...  4.52 us
    pallas_call x2, Pallas kernels, final_part(): pl.pallas_call(functools.partial(final_kernel, blocks, part), grid_spec=s...  3.94 us
    pallas_call x1, Pallas kernels, block_states(): pl.pallas_call(state_kernel, grid_spec=scalar_grid((2,), [source, source]...  2.79 us
  transfers between devices with their start and end apart: 16, of which 9 were waited for; matrix products, arithmetic and copies ran while one was open for 1% of the time, Pallas kernels for 25%

profile of v3, /device:TPU:0, one launch (start us, length us, event | category | flops | bytes accessed | tf_op | source)
XLA Modules:
  0.0 64.2 jit_solution(17674885895306459710)
XLA Ops:
  0.0 2.8 %states.1 = (bf16[16,128,128]{2,1,0:T(8,128)(2,1)S(1)}, bf16[16,128,128]{2,1,0:T(8,128)(2,1)S(1)}) custom-call(s32[1]{0:T(128)} %bitcast.place_ref, bf16[512,16,128]{2,1,0:T(8,128)(2,1)} %k_ref.5, bf16[512,16,128]{2,1,0:T(8,128)(2,1)} %v_ref.5), custom_call_target="tpu_custom_call" | custom-call | flops 268435456 | bytes 4194304 | tf_op jit(solution)/shard_map/states/pallas_call | solution.py:50
  2.8 0.0 copy-start
  2.9 3.0 %collective-permute-start = (bf16[4,128,128]{2,1,0:T(8,128)(2,1)S(1)}, bf16[4,128,128]{2,1,0:T(8,128)(2,1)S(1)}, u32[]{:S(2)}, u32[]{:S(2)}) collective-permute-start(bf16[4,128,128]{2,1,0:T(8,128)(2,1)S(1)} %get-tuple-element.33), channel_id=1, source_target_pairs={{0,1},{1,0},{2,3},{3,2},{4,5},{5,4},{6,7},{7,6},{8,9},{9,8},{10,11... | collective-permute-start | bytes 393224 | tf_op jit(solution)/shard_map/ppermute | solution.py:290
  5.9 1.5 %collective-permute-start.3 = (bf16[4,128,128]{2,1,0:T(8,128)(2,1)S(1)}, bf16[4,128,128]{2,1,0:T(8,128)(2,1)S(1)}, u32[]{:S(2)}, u32[]{:S(2)}) collective-permute-start(bf16[4,128,128]{2,1,0:T(8,128)(2,1)S(1)} %get-tuple-element.31), channel_id=1, source_target_pairs={{0,3},{1,2},{2,1},{3,0},{4,7},{5,6},{6,5},{7,4},{8,11},{9,10},{10,... | collective-permute-start | bytes 393224 | tf_op jit(solution)/shard_map/ppermute | solution.py:290
  7.4 0.0 collective-permute-start.2
  7.5 4.0 %collective-permute-done = bf16[4,128,128]{2,1,0:T(8,128)(2,1)S(1)} collective-permute-done((bf16[4,128,128]{2,1,0:T(8,128)(2,1)S(1)}, bf16[4,128,128]{2,1,0:T(8,128)(2,1)S(1)}, u32[]{:S(2)}, u32[]{:S(2)}) %collective-permute-start) | collective-permute-done | bytes 131104 | tf_op jit(solution)/shard_map/ppermute | solution.py:290
  11.5 1.7 %collective-permute-done.3 = bf16[4,128,128]{2,1,0:T(8,128)(2,1)S(1)} collective-permute-done((bf16[4,128,128]{2,1,0:T(8,128)(2,1)S(1)}, bf16[4,128,128]{2,1,0:T(8,128)(2,1)S(1)}, u32[]{:S(2)}, u32[]{:S(2)}) %collective-permute-start.3) | collective-permute-done | bytes 131104 | tf_op jit(solution)/shard_map/ppermute | solution.py:290
  13.2 0.4 collective-permute-done.2
  13.5 0.1 fusion.2
  13.6 2.8 %collective-permute-start.6 = (bf16[4,128,128]{2,1,0:T(8,128)(2,1)S(1)}, bf16[4,128,128]{2,1,0:T(8,128)(2,1)S(1)}, u32[]{:S(2)}, u32[]{:S(2)}) collective-permute-start(bf16[4,128,128]{2,1,0:T(8,128)(2,1)S(1)} %get-tuple-element.25), channel_id=1, source_target_pairs={{0,4},{1,5},{2,6},{3,7},{4,0},{5,1},{6,2},{7,3},{8,12},{9,13},{10,... | collective-permute-start | bytes 393224 | tf_op jit(solution)/shard_map/ppermute | solution.py:290
  16.5 5.4 %collective-permute-done.6 = bf16[4,128,128]{2,1,0:T(8,128)(2,1)S(1)} collective-permute-done((bf16[4,128,128]{2,1,0:T(8,128)(2,1)S(1)}, bf16[4,128,128]{2,1,0:T(8,128)(2,1)S(1)}, u32[]{:S(2)}, u32[]{:S(2)}) %collective-permute-start.6) | collective-permute-done | bytes 131104 | tf_op jit(solution)/shard_map/ppermute | solution.py:290
  21.9 0.1 collective-permute-start.9
  22.0 1.4 %collective-permute-start.1 = (bf16[12,128,128]{2,1,0:T(8,128)(2,1)S(1)}, bf16[12,128,128]{2,1,0:T(8,128)(2,1)S(1)}, u32[]{:S(2)}, u32[]{:S(2)}) collective-permute-start(bf16[12,128,128]{2,1,0:T(8,128)(2,1)S(1)} %pad_maximum_fusion.1), channel_id=1, source_target_pairs={{0,1},{1,0},{2,3},{3,2},{4,5},{5,4},{6,7},{7,6},{8,9},{9,8},{10,11... | collective-permute-start | bytes 1179656 | tf_op jit(solution)/shard_map/ppermute | solution.py:290
  23.4 0.0 copy-done
  23.4 6.1 %shard_map.46 = (f32[4,8,128,256]{3,2,1,0:T(8,128)}, bf16[4,8,256,128]{3,2,1,0:T(8,128)(2,1)}) custom-call(s32[1]{0:T(128)} %bitcast.place_ref, bf16[512,16,128]{2,1,0:T(8,128)(2,1)} %q_ref.3, bf16[512,16,128]{2,1,0:T(8,128)(2,1)} %k_ref.5, bf16[512,16,128]{2,1,0:T(8,128)(2,1)} %v_ref.5, f32[18,16,512]{2,1,0:T(8,128)S(1)} %copy-done, ...), custom_call_target="tpu_custom_call" | custom-call | flops 805306368 | bytes 9437184 | tf_op jit(solution)/shard_map/pallas_call | solution.py:136
  29.6 3.3 %shard_map.47 = (f32[4,8,128,256]{3,2,1,0:T(8,128)}, bf16[4,8,256,128]{3,2,1,0:T(8,128)(2,1)}) custom-call(s32[1]{0:T(128)} %bitcast.place_ref, bf16[512,16,128]{2,1,0:T(8,128)(2,1)} %q_ref.3, bf16[512,16,128]{2,1,0:T(8,128)(2,1)} %k_ref.5, bf16[512,16,128]{2,1,0:T(8,128)(2,1)} %v_ref.5, ...), custom_call_target="tpu_custom_call", output_to_operand_aliasing={{0}: (6, {}), {1}: (7, {})} | custom-call | flops 268435456 | bytes 3145728 | tf_op jit(solution)/shard_map/pallas_call | solution.py:136
  32.8 0.7 %collective-permute-start.4 = (bf16[4,128,128]{2,1,0:T(8,128)(2,1)S(1)}, bf16[4,128,128]{2,1,0:T(8,128)(2,1)S(1)}, u32[]{:S(2)}, u32[]{:S(2)}) collective-permute-start(bf16[4,128,128]{2,1,0:T(8,128)(2,1)S(1)} %get-tuple-element.24), channel_id=1, source_target_pairs={{0,1},{1,0},{2,3},{3,2},{4,5},{5,4},{6,7},{7,6},{8,9},{9,8},{10,11... | collective-permute-start | bytes 393224 | tf_op jit(solution)/shard_map/ppermute | solution.py:290
  33.5 0.0 collective-permute-done.9
  33.6 1.4 %collective-permute-start.10 = (bf16[4,128,128]{2,1,0:T(8,128)(2,1)S(1)}, bf16[4,128,128]{2,1,0:T(8,128)(2,1)S(1)}, u32[]{:S(2)}, u32[]{:S(2)}) collective-permute-start(bf16[4,128,128]{2,1,0:T(8,128)(2,1)S(1)} %add_convert_fusion), channel_id=1, source_target_pairs={{0,16},{1,17},{2,18},{3,19},{4,20},{5,21},{6,22},{7,23},{8,24},{9,... | collective-permute-start | bytes 393224 | tf_op jit(solution)/shard_map/ppermute | solution.py:290
  35.0 3.4 %collective-permute-done.4 = bf16[4,128,128]{2,1,0:T(8,128)(2,1)S(1)} collective-permute-done((bf16[4,128,128]{2,1,0:T(8,128)(2,1)S(1)}, bf16[4,128,128]{2,1,0:T(8,128)(2,1)S(1)}, u32[]{:S(2)}, u32[]{:S(2)}) %collective-permute-start.4) | collective-permute-done | bytes 131104 | tf_op jit(solution)/shard_map/ppermute | solution.py:290
  38.5 0.7 %collective-permute-start.5 = (bf16[8,128,128]{2,1,0:T(8,128)(2,1)S(1)}, bf16[8,128,128]{2,1,0:T(8,128)(2,1)S(1)}, u32[]{:S(2)}, u32[]{:S(2)}) collective-permute-start(bf16[8,128,128]{2,1,0:T(8,128)(2,1)S(1)} %constant_dynamic-update-slice_fusion.rest_0_), channel_id=1, source_target_pairs={{0,2},{1,3},{2,0},{3,1},{4,6},{5,7},{6,4},{7,5},{8,10},{9,11},{10,... | collective-permute-start | bytes 786440 | tf_op jit(solution)/shard_map/ppermute | solution.py:290
  39.2 0.5 collective-permute-start.7
  39.7 0.0 collective-permute-done.10
  39.8 1.6 %collective-permute-start.11 = (bf16[4,128,128]{2,1,0:T(8,128)(2,1)S(1)}, bf16[4,128,128]{2,1,0:T(8,128)(2,1)S(1)}, u32[]{:S(2)}, u32[]{:S(2)}) collective-permute-start(bf16[4,128,128]{2,1,0:T(8,128)(2,1)S(1)} %broadcast_select_fusion), channel_id=1, source_target_pairs={{0,2},{1,3},{2,0},{3,1},{4,6},{5,7},{6,4},{7,5},{8,10},{9,11},{10,... | collective-permute-start | bytes 393224 | tf_op jit(solution)/shard_map/ppermute | solution.py:290
  41.3 1.5 %collective-permute-start.12 = (bf16[4,128,128]{2,1,0:T(8,128)(2,1)S(1)}, bf16[4,128,128]{2,1,0:T(8,128)(2,1)S(1)}, u32[]{:S(2)}, u32[]{:S(2)}) collective-permute-start(bf16[4,128,128]{2,1,0:T(8,128)(2,1)S(1)} %broadcast_select_fusion), channel_id=1, source_target_pairs={{0,3},{1,2},{2,1},{3,0},{4,7},{5,6},{6,5},{7,4},{8,11},{9,10},{10,... | collective-permute-start | bytes 393224 | tf_op jit(solution)/shard_map/ppermute | solution.py:290
  42.9 1.3 %collective-permute-done.7 = bf16[4,128,128]{2,1,0:T(8,128)(2,1)S(1)} collective-permute-done((bf16[4,128,128]{2,1,0:T(8,128)(2,1)S(1)}, bf16[4,128,128]{2,1,0:T(8,128)(2,1)S(1)}, u32[]{:S(2)}, u32[]{:S(2)}) %collective-permute-start.7) | collective-permute-done | bytes 131104 | tf_op jit(solution)/shard_map/ppermute | solution.py:290
  44.2 1.4 %collective-permute-start.8 = (bf16[8,128,128]{2,1,0:T(8,128)(2,1)S(1)}, bf16[8,128,128]{2,1,0:T(8,128)(2,1)S(1)}, u32[]{:S(2)}, u32[]{:S(2)}) collective-permute-start(bf16[8,128,128]{2,1,0:T(8,128)(2,1)S(1)} %constant_dynamic-update-slice_fusion.2.rest_1_), channel_id=1, source_target_pairs={{0,2},{1,3},{2,0},{3,1},{4,6},{5,7},{6,4},{7,5},{8,10},{9,11},{10,... | collective-permute-start | bytes 786440 | tf_op jit(solution)/shard_map/ppermute | solution.py:290
  45.6 4.9 %collective-permute-done.11 = bf16[4,128,128]{2,1,0:T(8,128)(2,1)S(1)} collective-permute-done((bf16[4,128,128]{2,1,0:T(8,128)(2,1)S(1)}, bf16[4,128,128]{2,1,0:T(8,128)(2,1)S(1)}, u32[]{:S(2)}, u32[]{:S(2)}) %collective-permute-start.11) | collective-permute-done | bytes 131104 | tf_op jit(solution)/shard_map/ppermute | solution.py:290
  50.5 0.7 %collective-permute-start.14 = (bf16[4,128,128]{2,1,0:T(8,128)(2,1)S(1)}, bf16[4,128,128]{2,1,0:T(8,128)(2,1)S(1)}, u32[]{:S(2)}, u32[]{:S(2)}) collective-permute-start(bf16[4,128,128]{2,1,0:T(8,128)(2,1)S(1)} %broadcast_select_fusion), channel_id=1, source_target_pairs={{0,1},{1,0},{2,3},{3,2},{4,5},{5,4},{6,7},{7,6},{8,9},{9,8},{10,11... | collective-permute-start | bytes 393224 | tf_op jit(solution)/shard_map/ppermute | solution.py:290
  51.2 2.2 %collective-permute-done.12 = bf16[4,128,128]{2,1,0:T(8,128)(2,1)S(1)} collective-permute-done((bf16[4,128,128]{2,1,0:T(8,128)(2,1)S(1)}, bf16[4,128,128]{2,1,0:T(8,128)(2,1)S(1)}, u32[]{:S(2)}, u32[]{:S(2)}) %collective-permute-start.12) | collective-permute-done | bytes 131104 | tf_op jit(solution)/shard_map/ppermute | solution.py:290
  53.5 0.1 collective-permute-start.13
  53.5 2.0 %collective-permute-done.14 = bf16[4,128,128]{2,1,0:T(8,128)(2,1)S(1)} collective-permute-done((bf16[4,128,128]{2,1,0:T(8,128)(2,1)S(1)}, bf16[4,128,128]{2,1,0:T(8,128)(2,1)S(1)}, u32[]{:S(2)}, u32[]{:S(2)}) %collective-permute-start.14) | collective-permute-done | bytes 131104 | tf_op jit(solution)/shard_map/ppermute | solution.py:290
  55.5 0.1 collective-permute-start.15
  55.6 0.0 collective-permute-done.1
  55.6 0.1 pad_maximum_fusion.rest_0_
  55.7 4.5 %merge.1 = (f32[4,8,128,256]{3,2,1,0:T(8,128)S(1)}, bf16[4,8,512,256]{3,2,1,0:T(8,128)(2,1)S(1)}) custom-call(s32[1]{0:T(128)} %bitcast.place_ref, bf16[4,8,256,128]{3,2,1,0:T(8,128)(2,1)} %get-tuple-element.19.q_ref, f32[4,8,128,256]{3,2,1,0:T(8,128)} %get-tuple-element.20.a_ref, f32[18,16,512]{2,1,0:T(8,128)S(1)} %copy-done, ...), custom_call_target="tpu_custom_call" | custom-call | flops 268435456 | bytes 12582912 | tf_op jit(solution)/shard_map/merge/pallas_call | solution.py:217
  60.3 0.0 collective-permute-done.15.rest_3_
  60.3 2.0 %shard_map.48.rest_4_ = bf16[512,16,128]{2,1,0:T(8,128)(2,1)} custom-call(s32[1]{0:T(128)} %bitcast.place_ref, bf16[4,8,512,256]{3,2,1,0:T(8,128)(2,1)S(1)} %get-tuple-element.22.scaled_ref, f32[4,8,128,256]{3,2,1,0:T(8,128)S(1)} %get-tuple-element.23.a_ref, bf16[8,128,128]{2,1,0:T(8,128)(2,1)S(1)} %constant_dynamic-update-slice_fusion.rest_0_, ...), custom_call_target="tpu_custom_call" | custom-call | flops 536870912 | bytes 6291456 | tf_op jit(solution)/shard_map/pallas_call | solution.py:267
  62.2 0.0 collective-permute-done.5.rest_0_
  62.2 0.0 collective-permute-done.8.rest_1_
  62.2 0.0 collective-permute-done.13.rest_3_
  62.2 2.0 %shard_map.49 = bf16[512,16,128]{2,1,0:T(8,128)(2,1)} custom-call(s32[1]{0:T(128)} %bitcast.place_ref, bf16[4,8,512,256]{3,2,1,0:T(8,128)(2,1)S(1)} %get-tuple-element.22.scaled_ref, f32[4,8,128,256]{3,2,1,0:T(8,128)S(1)} %get-tuple-element.23.a_ref, bf16[8,128,128]{2,1,0:T(8,128)(2,1)S(1)} %collective-permute-done.5.rest_0_, ...), custom_call_target="tpu_custom_call", output_to_operand_aliasing={{}: (7, {})} | custom-call | flops 536870912 | bytes 6291456 | tf_op jit(solution)/shard_map/pallas_call | solution.py:267
  (14 shorter events, 0.3 us)
Async XLA Ops:
  2.8 20.6 %copy-start = (f32[18,16,512]{2,1,0:T(8,128)S(1)}, f32[18,16,512]{2,1,0:T(8,128)}, u32[]{:S(2)}) copy-start(f32[18,16,512]{2,1,0:T(8,128)} %w_ref.5) | copy-start | bytes 1769476
  2.9 8.6 %collective-permute-start = (bf16[4,128,128]{2,1,0:T(8,128)(2,1)S(1)}, bf16[4,128,128]{2,1,0:T(8,128)(2,1)S(1)}, u32[]{:S(2)}, u32[]{:S(2)}) collective-permute-start(bf16[4,128,128]{2,1,0:T(8,128)(2,1)S(1)} %get-tuple-element.33), channel_id=1, source_target_pairs={{0,1},{1,0},{2,3},{3,2},{4,5},{5,4},{6,7},{7,6},{8,9},{9,8},{10,11... | collective-permute-start | bytes 393224 | tf_op jit(solution)/shard_map/ppermute | solution.py:290
  5.9 7.3 %collective-permute-start.3 = (bf16[4,128,128]{2,1,0:T(8,128)(2,1)S(1)}, bf16[4,128,128]{2,1,0:T(8,128)(2,1)S(1)}, u32[]{:S(2)}, u32[]{:S(2)}) collective-permute-start(bf16[4,128,128]{2,1,0:T(8,128)(2,1)S(1)} %get-tuple-element.31), channel_id=1, source_target_pairs={{0,3},{1,2},{2,1},{3,0},{4,7},{5,6},{6,5},{7,4},{8,11},{9,10},{10,... | collective-permute-start | bytes 393224 | tf_op jit(solution)/shard_map/ppermute | solution.py:290
  7.4 6.1 %collective-permute-start.2 = (bf16[4,128,128]{2,1,0:T(8,128)(2,1)S(1)}, bf16[4,128,128]{2,1,0:T(8,128)(2,1)S(1)}, u32[]{:S(2)}, u32[]{:S(2)}) collective-permute-start(bf16[4,128,128]{2,1,0:T(8,128)(2,1)S(1)} %get-tuple-element.30), channel_id=1, source_target_pairs={{0,2},{1,3},{2,0},{3,1},{4,6},{5,7},{6,4},{7,5},{8,10},{9,11},{10,... | collective-permute-start | bytes 393224 | tf_op jit(solution)/shard_map/ppermute | solution.py:290
  13.6 8.2 %collective-permute-start.6 = (bf16[4,128,128]{2,1,0:T(8,128)(2,1)S(1)}, bf16[4,128,128]{2,1,0:T(8,128)(2,1)S(1)}, u32[]{:S(2)}, u32[]{:S(2)}) collective-permute-start(bf16[4,128,128]{2,1,0:T(8,128)(2,1)S(1)} %get-tuple-element.25), channel_id=1, source_target_pairs={{0,4},{1,5},{2,6},{3,7},{4,0},{5,1},{6,2},{7,3},{8,12},{9,13},{10,... | collective-permute-start | bytes 393224 | tf_op jit(solution)/shard_map/ppermute | solution.py:290
  21.9 11.6 %collective-permute-start.9 = (bf16[4,128,128]{2,1,0:T(8,128)(2,1)S(1)}, bf16[4,128,128]{2,1,0:T(8,128)(2,1)S(1)}, u32[]{:S(2)}, u32[]{:S(2)}) collective-permute-start(bf16[4,128,128]{2,1,0:T(8,128)(2,1)S(1)} %fusion.1), channel_id=1, source_target_pairs={{0,8},{1,9},{2,10},{3,11},{4,12},{5,13},{6,14},{7,15},{8,0},{9,1},... | collective-permute-start | bytes 393224 | tf_op jit(solution)/shard_map/ppermute | solution.py:290
  22.0 33.6 %collective-permute-start.1 = (bf16[12,128,128]{2,1,0:T(8,128)(2,1)S(1)}, bf16[12,128,128]{2,1,0:T(8,128)(2,1)S(1)}, u32[]{:S(2)}, u32[]{:S(2)}) collective-permute-start(bf16[12,128,128]{2,1,0:T(8,128)(2,1)S(1)} %pad_maximum_fusion.1), channel_id=1, source_target_pairs={{0,1},{1,0},{2,3},{3,2},{4,5},{5,4},{6,7},{7,6},{8,9},{9,8},{10,11... | collective-permute-start | bytes 1179656 | tf_op jit(solution)/shard_map/ppermute | solution.py:290
  32.8 5.6 %collective-permute-start.4 = (bf16[4,128,128]{2,1,0:T(8,128)(2,1)S(1)}, bf16[4,128,128]{2,1,0:T(8,128)(2,1)S(1)}, u32[]{:S(2)}, u32[]{:S(2)}) collective-permute-start(bf16[4,128,128]{2,1,0:T(8,128)(2,1)S(1)} %get-tuple-element.24), channel_id=1, source_target_pairs={{0,1},{1,0},{2,3},{3,2},{4,5},{5,4},{6,7},{7,6},{8,9},{9,8},{10,11... | collective-permute-start | bytes 393224 | tf_op jit(solution)/shard_map/ppermute | solution.py:290
  33.6 6.2 %collective-permute-start.10 = (bf16[4,128,128]{2,1,0:T(8,128)(2,1)S(1)}, bf16[4,128,128]{2,1,0:T(8,128)(2,1)S(1)}, u32[]{:S(2)}, u32[]{:S(2)}) collective-permute-start(bf16[4,128,128]{2,1,0:T(8,128)(2,1)S(1)} %add_convert_fusion), channel_id=1, source_target_pairs={{0,16},{1,17},{2,18},{3,19},{4,20},{5,21},{6,22},{7,23},{8,24},{9,... | collective-permute-start | bytes 393224 | tf_op jit(solution)/shard_map/ppermute | solution.py:290
  38.5 23.8 %collective-permute-start.5 = (bf16[8,128,128]{2,1,0:T(8,128)(2,1)S(1)}, bf16[8,128,128]{2,1,0:T(8,128)(2,1)S(1)}, u32[]{:S(2)}, u32[]{:S(2)}) collective-permute-start(bf16[8,128,128]{2,1,0:T(8,128)(2,1)S(1)} %constant_dynamic-update-slice_fusion.rest_0_), channel_id=1, source_target_pairs={{0,2},{1,3},{2,0},{3,1},{4,6},{5,7},{6,4},{7,5},{8,10},{9,11},{10,... | collective-permute-start | bytes 786440 | tf_op jit(solution)/shard_map/ppermute | solution.py:290
  39.2 5.0 %collective-permute-start.7 = (bf16[4,128,128]{2,1,0:T(8,128)(2,1)S(1)}, bf16[4,128,128]{2,1,0:T(8,128)(2,1)S(1)}, u32[]{:S(2)}, u32[]{:S(2)}) collective-permute-start(bf16[4,128,128]{2,1,0:T(8,128)(2,1)S(1)} %collective-permute-done.6), channel_id=1, source_target_pairs={{0,1},{1,0},{2,3},{3,2},{4,5},{5,4},{6,7},{7,6},{8,9},{9,8},{10,11... | collective-permute-start | bytes 393224 | tf_op jit(solution)/shard_map/ppermute | solution.py:290
  39.8 10.8 %collective-permute-start.11 = (bf16[4,128,128]{2,1,0:T(8,128)(2,1)S(1)}, bf16[4,128,128]{2,1,0:T(8,128)(2,1)S(1)}, u32[]{:S(2)}, u32[]{:S(2)}) collective-permute-start(bf16[4,128,128]{2,1,0:T(8,128)(2,1)S(1)} %broadcast_select_fusion), channel_id=1, source_target_pairs={{0,2},{1,3},{2,0},{3,1},{4,6},{5,7},{6,4},{7,5},{8,10},{9,11},{10,... | collective-permute-start | bytes 393224 | tf_op jit(solution)/shard_map/ppermute | solution.py:290
  41.3 12.1 %collective-permute-start.12 = (bf16[4,128,128]{2,1,0:T(8,128)(2,1)S(1)}, bf16[4,128,128]{2,1,0:T(8,128)(2,1)S(1)}, u32[]{:S(2)}, u32[]{:S(2)}) collective-permute-start(bf16[4,128,128]{2,1,0:T(8,128)(2,1)S(1)} %broadcast_select_fusion), channel_id=1, source_target_pairs={{0,3},{1,2},{2,1},{3,0},{4,7},{5,6},{6,5},{7,4},{8,11},{9,10},{10,... | collective-permute-start | bytes 393224 | tf_op jit(solution)/shard_map/ppermute | solution.py:290
  44.2 18.0 %collective-permute-start.8 = (bf16[8,128,128]{2,1,0:T(8,128)(2,1)S(1)}, bf16[8,128,128]{2,1,0:T(8,128)(2,1)S(1)}, u32[]{:S(2)}, u32[]{:S(2)}) collective-permute-start(bf16[8,128,128]{2,1,0:T(8,128)(2,1)S(1)} %constant_dynamic-update-slice_fusion.2.rest_1_), channel_id=1, source_target_pairs={{0,2},{1,3},{2,0},{3,1},{4,6},{5,7},{6,4},{7,5},{8,10},{9,11},{10,... | collective-permute-start | bytes 786440 | tf_op jit(solution)/shard_map/ppermute | solution.py:290
  50.5 5.0 %collective-permute-start.14 = (bf16[4,128,128]{2,1,0:T(8,128)(2,1)S(1)}, bf16[4,128,128]{2,1,0:T(8,128)(2,1)S(1)}, u32[]{:S(2)}, u32[]{:S(2)}) collective-permute-start(bf16[4,128,128]{2,1,0:T(8,128)(2,1)S(1)} %broadcast_select_fusion), channel_id=1, source_target_pairs={{0,1},{1,0},{2,3},{3,2},{4,5},{5,4},{6,7},{7,6},{8,9},{9,8},{10,11... | collective-permute-start | bytes 393224 | tf_op jit(solution)/shard_map/ppermute | solution.py:290
  53.5 8.8 %collective-permute-start.13 = (bf16[8,128,128]{2,1,0:T(8,128)(2,1)S(1)}, bf16[8,128,128]{2,1,0:T(8,128)(2,1)S(1)}, u32[]{:S(2)}, u32[]{:S(2)}) collective-permute-start(bf16[8,128,128]{2,1,0:T(8,128)(2,1)S(1)} %constant_dynamic-update-slice_fusion.4.rest_2_), channel_id=1, source_target_pairs={{0,8},{1,9},{2,10},{3,11},{4,12},{5,13},{6,14},{7,15},{8,0},{9,1},... | collective-permute-start | bytes 786440 | tf_op jit(solution)/shard_map/ppermute | solution.py:290
  55.5 4.7 %collective-permute-start.15 = (bf16[8,128,128]{2,1,0:T(8,128)(2,1)S(1)}, bf16[8,128,128]{2,1,0:T(8,128)(2,1)S(1)}, u32[]{:S(2)}, u32[]{:S(2)}) collective-permute-start(bf16[8,128,128]{2,1,0:T(8,128)(2,1)S(1)} %pad_maximum_fusion.2.rest_2_), channel_id=1, source_target_pairs={{0,8},{1,9},{2,10},{3,11},{4,12},{5,13},{6,14},{7,15},{8,0},{9,1},... | collective-permute-start | bytes 786440 | tf_op jit(solution)/shard_map/ppermute | solution.py:290
